TPU v7x, 256 devices: a whole 4x4x8 slice. The times are simulated.
256 devices in a mesh: cluster: 16 (over x, y), sub: 16 (over z, core).
Axes of the slice: x: 4, y: 4, z: 8, core: 2. Of those that a mesh axis runs over, the one named last changes fastest.
Arguments:
- dual_ops: float32 [16, 16, 1408, 1408], P('cluster', 'sub'), may hold values from -1 to 4.5, as said below
- contributions: float32 [16, 16, 1408, 64], P('cluster', 'sub'), may hold values from -6 to 6
- block_sizes: int32 [16, 16, 4], P('cluster', 'sub'), may hold values from 0 to 352, as said below
- mult_map: int32 [16, 16, 1408], P('cluster', 'sub'), may hold values from 0 to 1407, each once within a row
- coarse_basis: float32 [16, 16, 32, 704], P('cluster', 'sub'), may hold values from -0.21875 to 0.21875
- coarse_inverse: float32 [16, 512, 512], P('cluster'), may hold values from -0.1 to 0.5, as said below
Outputs:
- solution: float32 [16, 16, 1408, 64], P('cluster', 'sub')
- residual: float32 [16, 16, 1408, 64], P('cluster', 'sub')
Inputs may be any that keep to these rules, and one draw needn't show every extreme that they name: `dual_ops`: symmetric positive definite for each subdomain. block_sizes[c, s, k] equals the count on the facing side of the neighbour across side k; sides at the ends of an axis hold 0, all others 352 // 4 to 352; some side holds exactly 352. `mult_map`: for each subdomain a permutation of the 1408 slots. `coarse_inverse`: symmetric for each cluster.
All inputs are finite; a program needn't handle non-finite values.
Results may differ from a plain program's by a relative error of at most 0.0003.
Values sent between devices are 32-bit elements; how exact they have to be, the bound alone decides.
A program may use at most 64 MiB of HBM per device.

v0:
```python
import jax
import jax.numpy as jnp
from jax import lax
from jax.sharding import PartitionSpec as P

ITERS = 2


precise = lax.Precision.HIGHEST


def extended(value, sides, width):
    for axis, dim in sides:
        peers, length = (lax.axis_size(axis), value.shape[dim])
        up = [(i, (i + 1) % peers) for i in range(peers - 1)]
        down = [(j, i) for i, j in up]
        last = lax.slice_in_dim(value, length - width, length, axis=dim)
        leading = lax.slice_in_dim(value, 0, width, axis=dim)
        before = lax.ppermute(last, axis, up)
        after = lax.ppermute(leading, axis, down)
        value = jnp.concatenate([before, value, after], axis=dim)
    return value


def products(left, right):
    return lax.dot_general(
        left, right, (((0,), (0,)), ((), ())), precision=precise, preferred_element_type=jnp.float32
    )


def matmul(left, right):
    return jnp.dot(left, right, precision=precise, preferred_element_type=jnp.float32)


def chol_solve(factor, target):
    middle = lax.linalg.triangular_solve(factor, target, left_side=True, lower=True)
    return lax.linalg.triangular_solve(factor, middle, left_side=True, lower=True, transpose_a=True)


def join_pair(side_pair, padded):
    return jnp.stack([side_pair[0] + padded[0], side_pair[1] + padded[3]])


def shards(dual_ops, contributions, block_sizes, mult_map, coarse_basis, coarse_inverse):
    operator = dual_ops[0, 0]
    local_rhs = contributions[0, 0]
    side_sizes = block_sizes[0, 0]
    slot_map = mult_map[0, 0]
    basis_rows = coarse_basis[0, 0]
    coarse_matrix = coarse_inverse[0]
    orders = operator.shape[0]
    face_rows = orders // 4
    mode_count = basis_rows.shape[0]
    columns = local_rhs.shape[1]
    row_index = jnp.arange(orders, dtype=jnp.int32)
    row_side = row_index // face_rows
    row_place = row_index % face_rows
    side_match = row_side[:, None] == jnp.arange(4, dtype=jnp.int32)[None, :]
    row_limit = jnp.sum(jnp.where(side_match, side_sizes[None, :], 0), axis=1)
    live_rows = (row_place < row_limit).astype(jnp.float32)[:, None]
    row_weight = live_rows * jnp.where(row_side % 2 == 0, -1.0, 1.0).astype(jnp.float32)[:, None]
    inverse_map = jnp.argsort(slot_map)
    position = lax.axis_index("sub")
    lower_zeros = jnp.zeros((2 * face_rows, columns), jnp.float32)

    def assemble(values):
        blocks = (values * row_weight).reshape(4, face_rows, columns)
        along_sub = blocks[0:2]
        along_cluster = blocks[2:4]
        sub_halo = extended(along_sub, (("sub", 0),), 1)
        cluster_halo = extended(along_cluster, (("cluster", 0),), 1)
        joined = jnp.concatenate(
            [join_pair(along_sub, sub_halo), join_pair(along_cluster, cluster_halo)], axis=0
        )
        return joined.reshape(orders, columns) * live_rows

    selected = lax.dynamic_slice_in_dim(coarse_matrix, position * mode_count, mode_count, 0)

    def accumulate(piece_rows):
        return matmul(selected, piece_rows)

    def project(values):
        signed = (values * row_weight)[: 2 * face_rows]
        moments = matmul(basis_rows, signed)
        coefficients = accumulate(lax.all_gather(moments, "sub", axis=0, tiled=True))
        lifted = products(basis_rows, coefficients) * row_weight[: 2 * face_rows]
        side_pair = lifted.reshape(2, face_rows, columns)
        coarse_halo = extended(side_pair, (("sub", 0),), 1)
        upper = join_pair(side_pair, coarse_halo).reshape(2 * face_rows, columns)
        correction = jnp.concatenate([upper, lower_zeros], axis=0) * live_rows
        return values - correction

    residual = project(assemble(local_rhs))
    solution = jnp.zeros_like(residual)
    direction = residual
    for iteration in range(ITERS):
        local_vals = jnp.take(project(direction) * row_weight, slot_map, axis=0)
        mapped = matmul(operator, local_vals)
        mapped = project(assemble(jnp.take(mapped, inverse_map, axis=0)))
        curvature, descent = lax.psum(
            (0.5 * products(direction, mapped), 0.5 * products(direction, residual)),
            ("cluster", "sub"),
        )
        factor = jnp.linalg.cholesky(curvature)
        step_size = chol_solve(factor, descent)
        solution = solution + matmul(direction, step_size)
        residual = residual - matmul(mapped, step_size)
        if iteration + 1 < ITERS:
            coupling = lax.psum(0.5 * products(mapped, residual), ("cluster", "sub"))
            direction_mix = -chol_solve(factor, coupling)
            direction = residual + matmul(direction, direction_mix)
    return (solution[None, None], residual[None, None])


def solution(mesh):
    return jax.shard_map(
        shards,
        mesh=mesh,
        in_specs=(
            P("cluster", "sub", None, None),
            P("cluster", "sub", None, None),
            P("cluster", "sub", None),
            P("cluster", "sub", None),
            P("cluster", "sub", None, None),
            P("cluster", None, None),
        ),
        out_specs=(P("cluster", "sub", None, None), P("cluster", "sub", None, None)),
        check_vma=False,
    )
```

profile of v0, /device:TPU:1, one launch (start us, length us, event | category | flops | bytes accessed | tf_op | source)
XLA Modules:
  0.0 490.3 jit_solution(13150986672781962935)
XLA Ops:
  2.7 4.9 %collective-permute-start = (f32[1,352,64]{1,2,0:T(8,128)S(1)}, f32[1,352,64]{1,2,0:T(8,128)S(1)}, u32[]{:S(2)}, u32[]{:S(2)}) collective-permute-start(f32[1,352,64]{1,2,0:T(8,128)S(1)} %get-tuple-element.34), channel_id=1, source_target_pairs={{0,1},{1,2},{2,3},{3,4},{4,5},{5,6},{6,7},{7,8},{8,9},{9,10},{10,1... | collective-permute-start | bytes 270344 | tf_op jit(solution)/shard_map/ppermute | solution.py:19
  7.6 3.2 collective-permute-start.2
  10.9 1.3 collective-permute-start.3
  12.2 1.9 collective-permute-start.1
  14.9 5.0 %sort.17 = (s32[1408]{0:T(1024)}, s32[1408]{0:T(1024)S(1)}) sort(s32[1408]{0:T(1024)S(1)} %reduce.5, s32[1408]{0:T(1024)S(1)} %iota.76), dimensions={0}, to_apply=%region_1.3 | sort | flops 15488 | bytes 22528 | tf_op jit(solution)/shard_map/jit(argsort)/sort | solution.py:62
  22.0 20.7 %all_gather.15 = f32[512,64]{1,0:T(8,128)S(1)} all-gather(f32[32,64]{1,0:T(8,128)S(1)} %convolution_bitcast_fusion.4), channel_id=1, replica_groups=mesh['cluster'=16,'sub'=16] {'sub'}, dimensions={0}, use_global_device_ids=true | all-gather | bytes 139264 | tf_op jit(solution)/shard_map/all_gather | solution.py:85
  44.3 1.9 collective-permute-start.4
  46.2 2.4 collective-permute-start.5
  48.7 3.5 collective-permute-done.5
  53.0 15.7 %all_gather.16 = f32[512,64]{1,0:T(8,128)S(1)} all-gather(f32[32,64]{1,0:T(8,128)S(1)} %convolution_bitcast_fusion.3), channel_id=1, replica_groups=mesh['cluster'=16,'sub'=16] {'sub'}, dimensions={0}, use_global_device_ids=true | all-gather | bytes 139264 | tf_op jit(solution)/shard_map/all_gather | solution.py:85
  69.4 1.9 collective-permute-start.6
  71.4 2.4 collective-permute-start.7
  73.8 3.5 collective-permute-done.7
  78.1 2.7 gather_fusion
  80.8 10.9 %fusion.6 = f32[1408,64]{0,1:T(8,128)S(1)} fusion(f32[1,1,1408,1408]{3,2,1,0:T(8,128)} %param.13, f32[1408,64]{1,0:T(8,128)S(1)} %gather_fusion, pred[1408]{0:T(1024)(128)(4,1)S(1)} %compare_and_fusion.1), kind=kOutput, calls=%fused_computation.14 | convolution fusion | flops 1522622464 | bytes 8652160 | tf_op jit(solution)/shard_map/dot_general | solution.py:32
  91.9 2.7 gather_fusion.1
  95.1 1.9 collective-permute-start.8
  97.0 4.0 collective-permute-start.10
  102.3 2.7 collective-permute-start.9
  105.0 1.3 collective-permute-done.11
  106.3 1.9 collective-permute-done.9
  109.2 18.1 %all_gather.17 = f32[512,64]{1,0:T(8,128)S(1)} all-gather(f32[32,64]{1,0:T(8,128)S(1)} %convolution_bitcast_fusion.2), channel_id=1, replica_groups=mesh['cluster'=16,'sub'=16] {'sub'}, dimensions={0}, use_global_device_ids=true | all-gather | bytes 139264 | tf_op jit(solution)/shard_map/all_gather | solution.py:85
  128.0 2.2 collective-permute-start.12
  130.2 2.3 collective-permute-start.13
  133.0 3.1 collective-permute-done.13
  137.1 82.8 %all-reduce.6 = (f32[64,64]{0,1:T(8,128)S(1)}, f32[64,64]{0,1:T(8,128)S(1)}) all-reduce(f32[64,64]{0,1:T(8,128)S(1)} %convolution_multiply_fusion.8, f32[64,64]{0,1:T(8,128)S(1)} %convolution_multiply_fusion.9), channel_id=1, replica_groups=mesh['cluster'=16,'sub'=16] {'cluster','sub'}, use_global_device_ids=true, to_apply=%region_5.8 | all-reduce | flops 8192 | bytes 65536 | tf_op jit(solution)/shard_map/psum | solution.py:100
  220.0 5.8 %cholesky.44 = f32[64,64]{1,0:T(8,128)S(1)} custom-call(f32[64,64]{1,0:T(8,128)S(1)} %fusion.69), custom_call_target="Cholesky" | custom-call | tf_op jit(solution)/shard_map/jit(cholesky)/cholesky | solution.py:104
  227.2 4.9 custom-call.13
  233.5 72.9 %psum.37 = f32[64,64]{0,1:T(8,128)S(1)} all-reduce(f32[64,64]{0,1:T(8,128)S(1)} %convolution_multiply_fusion.7), channel_id=1, replica_groups=mesh['cluster'=16,'sub'=16] {'cluster','sub'}, use_global_device_ids=true, to_apply=%region_6.11 | all-reduce | flops 4096 | bytes 32768 | tf_op jit(solution)/shard_map/psum | solution.py:109
  307.6 17.4 %all_gather.18 = f32[512,64]{1,0:T(8,128)S(1)} all-gather(f32[32,64]{1,0:T(8,128)S(1)} %convolution_bitcast_fusion.1), channel_id=1, replica_groups=mesh['cluster'=16,'sub'=16] {'sub'}, dimensions={0}, use_global_device_ids=true | all-gather | bytes 139264 | tf_op jit(solution)/shard_map/all_gather | solution.py:85
  325.8 1.9 collective-permute-start.14
  327.7 2.6 collective-permute-start.15
  330.3 3.3 collective-permute-done.15
  334.4 3.6 gather_fusion.2
  338.1 11.0 %fusion.9 = f32[1408,64]{0,1:T(8,128)S(1)} fusion(f32[1,1,1408,1408]{3,2,1,0:T(8,128)} %param.13, f32[1408,64]{1,0:T(8,128)} %gather_fusion.2, pred[1408]{0:T(1024)(128)(4,1)S(1)} %compare_and_fusion.1), kind=kOutput, calls=%fused_computation.15 | convolution fusion | flops 1522622464 | bytes 8652160 | tf_op jit(solution)/shard_map/dot_general | solution.py:32
  349.4 3.6 gather_fusion.3
  353.0 1.4 copy.75
  354.6 1.9 collective-permute-start.16
  356.5 2.9 collective-permute-start.18
  360.7 2.7 collective-permute-start.17
  364.7 1.9 collective-permute-done.17
  367.6 17.8 %all_gather.19 = f32[512,64]{1,0:T(8,128)S(1)} all-gather(f32[32,64]{1,0:T(8,128)S(1)} %convolution_bitcast_fusion), channel_id=1, replica_groups=mesh['cluster'=16,'sub'=16] {'sub'}, dimensions={0}, use_global_device_ids=true | all-gather | bytes 139264 | tf_op jit(solution)/shard_map/all_gather | solution.py:85
  386.1 2.1 collective-permute-start.20
  388.2 2.2 collective-permute-start.21
  391.0 3.2 collective-permute-done.21
  395.1 80.1 %all-reduce.5 = (f32[64,64]{0,1:T(8,128)S(1)}, f32[64,64]{0,1:T(8,128)S(1)}) all-reduce(f32[64,64]{0,1:T(8,128)S(1)} %convolution_multiply_fusion.5, f32[64,64]{0,1:T(8,128)S(1)} %convolution_multiply_fusion.6), channel_id=1, replica_groups=mesh['cluster'=16,'sub'=16] {'cluster','sub'}, use_global_device_ids=true, to_apply=%region_8.13 | all-reduce | flops 8192 | bytes 65536 | tf_op jit(solution)/shard_map/psum | solution.py:100
  475.3 5.8 %cholesky.55 = f32[64,64]{1,0:T(8,128)S(1)} custom-call(f32[64,64]{1,0:T(8,128)S(1)} %fusion.61), custom_call_target="Cholesky" | custom-call | tf_op jit(solution)/shard_map/jit(cholesky)/cholesky | solution.py:104
  482.5 4.9 custom-call.17
  (132 shorter events, 29.6 us)
Async XLA Ops:
  0.6 42.1 %copy-start = (f32[1,512,512]{2,1,0:T(8,128)S(1)}, f32[1,512,512]{2,1,0:T(8,128)}, u32[]{:S(2)}) copy-start(f32[1,512,512]{2,1,0:T(8,128)} %param.18) | copy-start | bytes 3145732
  0.6 52.0 %copy-start.1 = (f32[1,1,32,704]{3,2,1,0:T(8,128)S(1)}, f32[1,1,32,704]{3,2,1,0:T(8,128)}, u32[]{:S(2)}) copy-start(f32[1,1,32,704]{3,2,1,0:T(8,128)} %param.17) | copy-start | bytes 270340
  2.7 17.3 %collective-permute-start = (f32[1,352,64]{1,2,0:T(8,128)S(1)}, f32[1,352,64]{1,2,0:T(8,128)S(1)}, u32[]{:S(2)}, u32[]{:S(2)}) collective-permute-start(f32[1,352,64]{1,2,0:T(8,128)S(1)} %get-tuple-element.34), channel_id=1, source_target_pairs={{0,1},{1,2},{2,3},{3,4},{4,5},{5,6},{6,7},{7,8},{8,9},{9,10},{10,1... | collective-permute-start | bytes 270344 | tf_op jit(solution)/shard_map/ppermute | solution.py:19
  7.6 12.4 %collective-permute-start.2 = (f32[1,352,64]{1,2,0:T(8,128)S(1)}, f32[1,352,64]{1,2,0:T(8,128)S(1)}, u32[]{:S(2)}, u32[]{:S(2)}) collective-permute-start(f32[1,352,64]{1,2,0:T(8,128)S(1)} %get-tuple-element.35), channel_id=1, source_target_pairs={{0,16},{16,32},{32,48},{48,64},{64,80},{80,96},{96,112},{112,128},... | collective-permute-start | bytes 270344 | tf_op jit(solution)/shard_map/ppermute | solution.py:19
  10.9 9.2 %collective-permute-start.3 = (f32[1,352,64]{1,2,0:T(8,128)S(1)}, f32[1,352,64]{1,2,0:T(8,128)S(1)}, u32[]{:S(2)}, u32[]{:S(2)}) collective-permute-start(f32[1,352,64]{1,2,0:T(8,128)S(1)} %get-tuple-element.36), channel_id=1, source_target_pairs={{16,0},{32,16},{48,32},{64,48},{80,64},{96,80},{112,96},{128,112},... | collective-permute-start | bytes 270344 | tf_op jit(solution)/shard_map/ppermute | solution.py:20
  12.2 7.9 %collective-permute-start.1 = (f32[1,352,64]{1,2,0:T(8,128)S(1)}, f32[1,352,64]{1,2,0:T(8,128)S(1)}, u32[]{:S(2)}, u32[]{:S(2)}) collective-permute-start(f32[1,352,64]{1,2,0:T(8,128)S(1)} %get-tuple-element.37), channel_id=1, source_target_pairs={{1,0},{2,1},{3,2},{4,3},{5,4},{6,5},{7,6},{8,7},{9,8},{10,9},{11,1... | collective-permute-start | bytes 270344 | tf_op jit(solution)/shard_map/ppermute | solution.py:20
  44.3 4.4 collective-permute-start.4
  46.2 5.9 %collective-permute-start.5 = (f32[1,352,64]{1,2,0:T(8,128)S(1)}, f32[1,352,64]{1,2,0:T(8,128)S(1)}, u32[]{:S(2)}, u32[]{:S(2)}) collective-permute-start(f32[1,352,64]{1,2,0:T(8,128)S(1)} %get-tuple-element.57), channel_id=1, source_target_pairs={{1,0},{2,1},{3,2},{4,3},{5,4},{6,5},{7,6},{8,7},{9,8},{10,9},{11,1... | collective-permute-start | bytes 270344 | tf_op jit(solution)/shard_map/ppermute | solution.py:20
  69.4 4.4 collective-permute-start.6
  71.4 5.9 %collective-permute-start.7 = (f32[1,352,64]{1,2,0:T(8,128)S(1)}, f32[1,352,64]{1,2,0:T(8,128)S(1)}, u32[]{:S(2)}, u32[]{:S(2)}) collective-permute-start(f32[1,352,64]{1,2,0:T(8,128)S(1)} %get-tuple-element.53), channel_id=1, source_target_pairs={{1,0},{2,1},{3,2},{4,3},{5,4},{6,5},{7,6},{8,7},{9,8},{10,9},{11,1... | collective-permute-start | bytes 270344 | tf_op jit(solution)/shard_map/ppermute | solution.py:20
  95.1 9.9 %collective-permute-start.8 = (f32[1,352,64]{1,2,0:T(8,128)S(1)}, f32[1,352,64]{1,2,0:T(8,128)S(1)}, u32[]{:S(2)}, u32[]{:S(2)}) collective-permute-start(f32[1,352,64]{1,2,0:T(8,128)S(1)} %get-tuple-element.26), channel_id=1, source_target_pairs={{0,1},{1,2},{2,3},{3,4},{4,5},{5,6},{6,7},{7,8},{8,9},{9,10},{10,1... | collective-permute-start | bytes 270344 | tf_op jit(solution)/shard_map/ppermute | solution.py:19
  97.0 8.0 %collective-permute-start.10 = (f32[1,352,64]{1,2,0:T(8,128)S(1)}, f32[1,352,64]{1,2,0:T(8,128)S(1)}, u32[]{:S(2)}, u32[]{:S(2)}) collective-permute-start(f32[1,352,64]{1,2,0:T(8,128)S(1)} %get-tuple-element.27), channel_id=1, source_target_pairs={{0,16},{16,32},{32,48},{48,64},{64,80},{80,96},{96,112},{112,128},... | collective-permute-start | bytes 270344 | tf_op jit(solution)/shard_map/ppermute | solution.py:19
  101.0 5.4 %collective-permute-start.11 = (f32[1,352,64]{1,2,0:T(8,128)S(1)}, f32[1,352,64]{1,2,0:T(8,128)S(1)}, u32[]{:S(2)}, u32[]{:S(2)}) collective-permute-start(f32[1,352,64]{1,2,0:T(8,128)S(1)} %get-tuple-element.28), channel_id=1, source_target_pairs={{16,0},{32,16},{48,32},{64,48},{80,64},{96,80},{112,96},{128,112},... | collective-permute-start | bytes 270344 | tf_op jit(solution)/shard_map/ppermute | solution.py:20
  102.3 5.9 %collective-permute-start.9 = (f32[1,352,64]{1,2,0:T(8,128)S(1)}, f32[1,352,64]{1,2,0:T(8,128)S(1)}, u32[]{:S(2)}, u32[]{:S(2)}) collective-permute-start(f32[1,352,64]{1,2,0:T(8,128)S(1)} %get-tuple-element.29), channel_id=1, source_target_pairs={{1,0},{2,1},{3,2},{4,3},{5,4},{6,5},{7,6},{8,7},{9,8},{10,9},{11,1... | collective-permute-start | bytes 270344 | tf_op jit(solution)/shard_map/ppermute | solution.py:20
  128.0 5.0 %collective-permute-start.12 = (f32[1,352,64]{1,2,0:T(8,128)S(1)}, f32[1,352,64]{1,2,0:T(8,128)S(1)}, u32[]{:S(2)}, u32[]{:S(2)}) collective-permute-start(f32[1,352,64]{1,2,0:T(8,128)S(1)} %get-tuple-element.48), channel_id=1, source_target_pairs={{0,1},{1,2},{2,3},{3,4},{4,5},{5,6},{6,7},{7,8},{8,9},{9,10},{10,1... | collective-permute-start | bytes 270344 | tf_op jit(solution)/shard_map/ppermute | solution.py:19
  130.2 5.9 %collective-permute-start.13 = (f32[1,352,64]{1,2,0:T(8,128)S(1)}, f32[1,352,64]{1,2,0:T(8,128)S(1)}, u32[]{:S(2)}, u32[]{:S(2)}) collective-permute-start(f32[1,352,64]{1,2,0:T(8,128)S(1)} %get-tuple-element.49), channel_id=1, source_target_pairs={{1,0},{2,1},{3,2},{4,3},{5,4},{6,5},{7,6},{8,7},{9,8},{10,9},{11,1... | collective-permute-start | bytes 270344 | tf_op jit(solution)/shard_map/ppermute | solution.py:20
  325.8 4.6 collective-permute-start.14
  327.7 5.9 %collective-permute-start.15 = (f32[1,352,64]{1,2,0:T(8,128)S(1)}, f32[1,352,64]{1,2,0:T(8,128)S(1)}, u32[]{:S(2)}, u32[]{:S(2)}) collective-permute-start(f32[1,352,64]{1,2,0:T(8,128)S(1)} %get-tuple-element.45), channel_id=1, source_target_pairs={{1,0},{2,1},{3,2},{4,3},{5,4},{6,5},{7,6},{8,7},{9,8},{10,9},{11,1... | collective-permute-start | bytes 270344 | tf_op jit(solution)/shard_map/ppermute | solution.py:20
  354.6 9.3 %collective-permute-start.16 = (f32[1,352,64]{1,2,0:T(8,128)S(1)}, f32[1,352,64]{1,2,0:T(8,128)S(1)}, u32[]{:S(2)}, u32[]{:S(2)}) collective-permute-start(f32[1,352,64]{1,2,0:T(8,128)S(1)} %get-tuple-element.18), channel_id=1, source_target_pairs={{0,1},{1,2},{2,3},{3,4},{4,5},{5,6},{6,7},{7,8},{8,9},{9,10},{10,1... | collective-permute-start | bytes 270344 | tf_op jit(solution)/shard_map/ppermute | solution.py:19
  356.5 7.4 %collective-permute-start.18 = (f32[1,352,64]{1,2,0:T(8,128)S(1)}, f32[1,352,64]{1,2,0:T(8,128)S(1)}, u32[]{:S(2)}, u32[]{:S(2)}) collective-permute-start(f32[1,352,64]{1,2,0:T(8,128)S(1)} %get-tuple-element.19), channel_id=1, source_target_pairs={{0,16},{16,32},{32,48},{48,64},{64,80},{80,96},{96,112},{112,128},... | collective-permute-start | bytes 270344 | tf_op jit(solution)/shard_map/ppermute | solution.py:19
  359.4 5.4 %collective-permute-start.19 = (f32[1,352,64]{1,2,0:T(8,128)S(1)}, f32[1,352,64]{1,2,0:T(8,128)S(1)}, u32[]{:S(2)}, u32[]{:S(2)}) collective-permute-start(f32[1,352,64]{1,2,0:T(8,128)S(1)} %get-tuple-element.20), channel_id=1, source_target_pairs={{16,0},{32,16},{48,32},{64,48},{80,64},{96,80},{112,96},{128,112},... | collective-permute-start | bytes 270344 | tf_op jit(solution)/shard_map/ppermute | solution.py:20
  360.7 5.9 %collective-permute-start.17 = (f32[1,352,64]{1,2,0:T(8,128)S(1)}, f32[1,352,64]{1,2,0:T(8,128)S(1)}, u32[]{:S(2)}, u32[]{:S(2)}) collective-permute-start(f32[1,352,64]{1,2,0:T(8,128)S(1)} %get-tuple-element.21), channel_id=1, source_target_pairs={{1,0},{2,1},{3,2},{4,3},{5,4},{6,5},{7,6},{8,7},{9,8},{10,9},{11,1... | collective-permute-start | bytes 270344 | tf_op jit(solution)/shard_map/ppermute | solution.py:20
  386.1 4.8 collective-permute-start.20
  388.2 5.9 %collective-permute-start.21 = (f32[1,352,64]{1,2,0:T(8,128)S(1)}, f32[1,352,64]{1,2,0:T(8,128)S(1)}, u32[]{:S(2)}, u32[]{:S(2)}) collective-permute-start(f32[1,352,64]{1,2,0:T(8,128)S(1)} %get-tuple-element.41), channel_id=1, source_target_pairs={{1,0},{2,1},{3,2},{4,3},{5,4},{6,5},{7,6},{8,7},{9,8},{10,9},{11,1... | collective-permute-start | bytes 270344 | tf_op jit(solution)/shard_map/ppermute | solution.py:20
where the time goes:
time: 492 us; the launch traced here: 490 us
  blocking collectives  326 us (66%)
  starting transfers between devices  52 us (11%)
  matrix products  35.9 us (7%)
  other arithmetic  33.3 us (7%)
  waiting for transfers between devices  22.5 us (5%)
  local copies, waits for them, and re-layouts  19.4 us (4%)
    psum x2, blocking collectives, shards(): lax.psum((0.5 * products(direction, mapped), 0.5 * products(direction, re...  163 us
    all_gather x5, blocking collectives, project(): lax.all_gather(moments, 'sub', axis=0, tiled=True)  89.7 us
    psum x1, blocking collectives, shards(): coupling = lax.psum(0.5 * products(mapped, residual), ('cluster', 'sub'))  72.9 us
    dot_general x17, matrix products, matmul(): jnp.dot(left, right, precision=precise, preferred_element_type=jnp.float32)  29.5 us
    ppermute x11, starting transfers between devices, extended(): before = lax.ppermute(last, axis, up)  28.8 us
    ppermute x11, starting transfers between devices, extended(): after = lax.ppermute(leading, axis, down)  23.2 us
    ppermute x11, waiting for transfers between devices, extended(): after = lax.ppermute(leading, axis, down)  22.5 us
    another operation x6, other arithmetic, shards(): factor = jnp.linalg.cholesky(curvature)  13 us
  transfers between devices with their start and end apart: 22, of which 9 were waited for; matrix products, arithmetic and copies ran while one was open for 1% of the time, Pallas kernels for 0%

commit v1 on v0

v1 whole, which is shorter than its diff:
```python
import jax
import jax.numpy as jnp
from jax import lax
from jax.sharding import PartitionSpec as P
from jax.experimental import pallas as pl
from jax.experimental.pallas import tpu as pltpu


ROWS = 1408
FACE = 352
SIDE = 384
WIDE = 4 * SIDE
PAIR = 2 * SIDE
COLS = 64
MODES = 32
SUBS = 16
COARSE = 512
SIGNS = (-1.0, 1.0, -1.0, 1.0)
FACING = (1, 0, 3, 2)

F32 = jnp.float32
BF16 = jnp.bfloat16
NN = (((1,), (0,)), ((), ()))
NT = (((1,), (1,)), ((), ()))


def exact(left, right, dims=NN):
    return lax.dot_general(
        left, right, dims, precision=lax.Precision.HIGHEST, preferred_element_type=F32
    )


def single(left, right):
    return lax.dot_general(left, right, NN, preferred_element_type=F32)


def split(value):
    high = value.astype(BF16)
    return high, (value - high.astype(F32)).astype(BF16)


def fold(value):
    half = value.shape[0] // 2
    return jnp.concatenate([value[:half], value[half:]], axis=1)


def unfold(value):
    half = value.shape[1] // 2
    return jnp.concatenate([value[:, :half], value[:, half:]], axis=0)


def part(side):
    return slice(side * SIDE, (side + 1) * SIDE)


def kernel(
    ops_hbm, contrib_hbm, sizes, map_ref, basis_hbm, coarse_hbm,
    sol_hbm, res_hbm,
    full, high, low, scatter, gather,
    own_rhs, halo_rhs, own_basis, near_basis, coarse, moments_map,
    weights, first, dirs, resid, proj, image, image_proj, local,
    halo_one, halo_two, near_one, near_two, out_one, out_two, far_one, far_two,
    all_q, all_m, all_one, all_two, mixed, table_even, table_odd, dense_m,
    sum_a, sum_b, sum_c, square, out_sol, out_res,
    local_sem, send_sem, recv_sem,
):
    c, s = lax.axis_index("cluster"), lax.axis_index("sub")
    x, y = lax.div(c, 4), lax.rem(c, 4)
    z, core = lax.div(s, 2), lax.rem(s, 2)
    down, up = lax.rem(s + SUBS - 1, SUBS), lax.rem(s + 1, SUBS)
    west, east = lax.rem(c + 15, 16), lax.rem(c + 1, 16)
    mate = z * 2 + 1 - core
    x_peers = [(lax.rem(x + i, 4) * 4 + y, s) for i in range(1, 4)]
    y_peers = [(x * 4 + lax.rem(y + i, 4), s) for i in range(1, 4)]
    z_peers = [(c, lax.rem(z + i, 8) * 2 + core) for i in range(1, 8)]
    side_peers = ((c, down), (c, up), (west, s), (east, s))
    used = [0]

    def fresh():
        used[0] += 1
        return used[0] - 1

    loads = [
        pltpu.make_async_copy(contrib_hbm.at[0, 0], own_rhs, local_sem.at[0]),
        pltpu.make_async_copy(basis_hbm.at[0, 0], own_basis, local_sem.at[1]),
        pltpu.make_async_copy(
            coarse_hbm.at[0], coarse.at[pl.ds(MODES, COARSE)], local_sem.at[2]
        ),
        pltpu.make_async_copy(ops_hbm.at[0, 0], full, local_sem.at[3]),
    ]
    for load in loads:
        load.start()

    barrier = pltpu.get_barrier_semaphore()
    greeted = [(c, mate)] + z_peers + x_peers + y_peers
    greeted += [(c, down), (c, up), (west, s), (east, s)]
    for peer in greeted:
        pl.semaphore_signal(
            barrier, inc=1, device_id=peer, device_id_type=pl.DeviceIdType.MESH
        )
    pl.semaphore_wait(barrier, len(greeted))

    def send(source, target, peer, slot):
        copy = pltpu.make_async_remote_copy(
            src_ref=source, dst_ref=target,
            send_sem=send_sem.at[slot], recv_sem=recv_sem.at[slot],
            device_id=peer, device_id_type=pl.DeviceIdType.MESH,
        )
        copy.start()
        return copy

    pending = []

    def share(buffer, me, peers):
        slot = fresh()
        for peer in peers:
            send(buffer.at[me], buffer.at[me], peer, slot)
        whole = buffer.at[pl.ds(0, len(peers))]
        pending.append(lambda: pltpu.make_async_copy(whole, whole, send_sem.at[slot]).wait())
        return pltpu.make_async_copy(whole, whole, recv_sem.at[slot])

    def swap(source, target, peer):
        copy = send(source, target, peer, fresh())
        pending.append(copy.wait_send)
        return copy

    rhs_copies = [
        swap(
            contrib_hbm.at[0, 0, pl.ds(side * FACE, FACE)],
            halo_rhs.at[FACING[side]], side_peers[side],
        )
        for side in range(4)
    ]
    basis_copies = [
        swap(basis_hbm.at[0, 0], near_basis.at[1], (c, down)),
        swap(basis_hbm.at[0, 0], near_basis.at[0], (c, up)),
    ]

    slots = map_ref[0]
    slots = slots + (SIDE - FACE) * (
        (slots >= FACE).astype(jnp.int32)
        + (slots >= 2 * FACE).astype(jnp.int32)
        + (slots >= 3 * FACE).astype(jnp.int32)
    )

    def fill_scatter(step, carry):
        rows = pl.ds(pl.multiple_of(step * 128, 128), 128)
        index = lax.broadcasted_iota(jnp.int32, (128, ROWS), 0) + step * 128
        scatter[rows, :] = jnp.where(index == slots, 1.0, 0.0).astype(BF16)
        return carry

    lax.fori_loop(0, WIDE // 128, fill_scatter, 0)
    columns = lax.broadcasted_iota(jnp.int32, (128, 128), 1).astype(F32)
    for step in range(ROWS // 128):
        piece = slots[:, step * 128 : (step + 1) * 128].astype(F32)
        tall = jnp.broadcast_to(piece, (128, 128)).T
        for tile in range(WIDE // 128):
            gather[step * 128 : (step + 1) * 128, tile * 128 : (tile + 1) * 128] = (
                jnp.where(tall == columns + float(tile * 128), 1.0, 0.0).astype(BF16)
            )

    lanes = lax.broadcasted_iota(jnp.int32, (8, SIDE), 1)
    for side in range(4):
        weights[:, part(side)] = jnp.where(lanes < sizes[0, 0, side], SIGNS[side], 0.0)

    loads[1].wait()
    zero_lanes = jnp.zeros((MODES, SIDE - FACE), F32)

    def half_basis(value, side):
        return jnp.concatenate(
            [value[:, side * FACE : (side + 1) * FACE], zero_lanes], axis=1
        )

    weight_low, weight_high = weights[0:1, part(0)], weights[0:1, part(1)]
    empty = jnp.zeros((MODES, SIDE), F32)
    mine = own_basis[...]
    moments_map[MODES : 2 * MODES, part(0)] = half_basis(mine, 0) * weight_low
    moments_map[MODES : 2 * MODES, part(1)] = half_basis(mine, 1) * weight_high
    for copy in basis_copies:
        copy.wait_recv()
    moments_map[0:MODES, part(0)] = -half_basis(near_basis[0], 1) * weight_low
    moments_map[0:MODES, part(1)] = empty
    moments_map[2 * MODES : 3 * MODES, part(0)] = empty
    moments_map[2 * MODES : 3 * MODES, part(1)] = (
        -half_basis(near_basis[1], 0) * weight_high
    )
    moments_map[3 * MODES : 4 * MODES, :] = jnp.zeros((MODES, PAIR), F32)

    def gather_start(buffer, value):
        buffer[core, z] = value
        return share(buffer.at[core], z, z_peers)

    def gather_finish(buffer, arrived):
        arrived.wait()
        return swap(buffer.at[core], buffer.at[core], (c, mate))

    m_own = exact(moments_map[MODES : 2 * MODES, :], moments_map[...], NT)
    m_arrived = gather_start(all_m, m_own)

    loads[0].wait()
    for copy in rhs_copies:
        copy.wait_recv()
    index = lax.broadcasted_iota(jnp.int32, (FACE, COLS), 0)
    zero_rows = jnp.zeros((SIDE - FACE, COLS), F32)
    for side in range(4):
        own = own_rhs[side * FACE : (side + 1) * FACE, :]
        joined = jnp.where(
            index < sizes[0, 0, side], SIGNS[side] * (own - halo_rhs[side]), 0.0
        )
        first[:, part(side)] = jnp.concatenate([joined, zero_rows], axis=0).T
    q_moments = exact(moments_map[MODES : 2 * MODES, :], first[:, :PAIR], NT)
    q_arrived = gather_start(all_q, fold(q_moments))

    loads[3].wait()

    def split_rows(step, carry):
        rows = pl.ds(pl.multiple_of(step * 64, 64), 64)
        high[rows, :], low[rows, :] = split(full[rows, :])
        return carry

    loads[2].wait()
    coarse[0:MODES, :] = jnp.zeros((MODES, COARSE), F32)
    coarse[MODES + COARSE :, :] = jnp.zeros((2 * MODES, COARSE), F32)
    near_rows = coarse[pl.ds(pl.multiple_of(s * MODES, MODES), 4 * MODES), :]
    near = near_rows.T

    m_crossed = gather_finish(all_m, m_arrived)
    q_crossed = gather_finish(all_q, q_arrived)
    lax.fori_loop(0, ROWS // 64, split_rows, 0)
    m_crossed.wait_recv()
    dense_m[...] = jnp.zeros((COARSE, COARSE + 256), F32)
    for block in range(SUBS):
        offset = 32 * (block - 1) + 128
        tile, shift = offset // 128, offset % 128
        rows = slice(block * MODES, (block + 1) * MODES)
        value = all_m[block % 2, block // 2]
        if shift:
            value = pltpu.roll(value, shift, 1)
        lane = lax.broadcasted_iota(jnp.int32, (MODES, 128), 1)
        dense_m[rows, tile * 128 : (tile + 1) * 128] = jnp.where(lane >= shift, value, 0.0)
        if shift:
            dense_m[rows, (tile + 1) * 128 : (tile + 2) * 128] = jnp.where(
                lane < shift, value, 0.0
            )
    square_m = dense_m[:, 128 : 128 + COARSE]
    inner = coarse[MODES : MODES + COARSE, :]
    mixed[:, 0:128] = near
    mixed[:, 128:256] = near - exact(inner, exact(square_m, near))
    for block in range(SUBS):
        to = ((block % 2) * 8 + block // 2) * 16
        table_even[to : to + 16, :] = mixed[block * MODES : block * MODES + 16, :]
        table_odd[to : to + 16, :] = mixed[block * MODES + 16 : (block + 1) * MODES, :]

    def coefficients(buffer):
        turned = buffer[...].reshape(SUBS * 16, 128).T
        return exact(turned[:COLS], table_even[...]) + exact(
            turned[COLS:], table_odd[...]
        )

    def project_pair(value, value_proj, factors, source):
        lift = exact(
            jnp.concatenate([factors[:, :128], factors[:, 128:]], axis=0),
            moments_map[...],
        )
        once = source[:, :PAIR] - lift[:COLS]
        value[:, :PAIR] = once
        value_proj[:, :PAIR] = once - lift[COLS:]
        value[:, PAIR:] = source[:, PAIR:]
        value_proj[:, PAIR:] = source[:, PAIR:]

    q_crossed.wait_recv()
    project_pair(dirs, proj, coefficients(all_q), first)

    def reduce_all(bufs, value):
        mates, along_x, along_y, along_z, halves = bufs
        rows = value.shape[0] // 2
        mates[core, 0] = value[:rows]
        mates[core, 1] = value[rows:]
        copy = swap(mates.at[core, 1 - core], mates.at[core, 1 - core], (c, mate))
        yield
        copy.wait_recv()
        along_x[x] = mates[0, core] + mates[1, core]
        arrived = share(along_x, x, x_peers)
        yield
        arrived.wait()
        along_y[y] = (along_x[0] + along_x[1]) + (along_x[2] + along_x[3])
        arrived = share(along_y, y, y_peers)
        yield
        arrived.wait()
        along_z[z] = (along_y[0] + along_y[1]) + (along_y[2] + along_y[3])
        arrived = share(along_z, z, z_peers)
        yield
        arrived.wait()
        total = along_z[0]
        for i in range(1, 8):
            total = total + along_z[i]
        halves[core] = total
        copy = swap(halves.at[core], halves.at[core], (c, mate))
        yield
        copy.wait_recv()
        yield jnp.concatenate([halves[0], halves[1]], axis=0)

    def dual(source, halos, outs, nears, sides_out, alls):
        high_x, low_x = split(source[...] * weights[0:1, :])
        both = single(jnp.concatenate([high_x, low_x], axis=0), scatter[...]).astype(BF16)
        turned = single(both, high[...])
        image_local = turned[:COLS] + turned[COLS:] + single(both[:COLS], low[...])
        high_f, low_f = split(image_local)
        back = single(jnp.concatenate([high_f, low_f], axis=0), gather[...])
        back = (back[:COLS] + back[COLS:]) * weights[0:1, :]
        halo_copies = []
        for side in range(4):
            sides_out[side] = back[:, part(side)]
        shares = exact(moments_map[...], back[:, :PAIR], NT)
        outs[0] = fold(shares[0:MODES])
        outs[1] = fold(shares[2 * MODES : 3 * MODES])
        near_copies = [
            swap(outs.at[0], nears.at[1], (c, down)),
            swap(outs.at[1], nears.at[0], (c, up)),
        ]
        for side in range(4):
            halo_copies.append(
                swap(sides_out.at[side], halos.at[FACING[side]], side_peers[side])
            )
        energy = exact(
            both[:COLS].astype(F32) + both[COLS:].astype(F32), image_local, NT
        )
        return energy, fold(shares[MODES : 2 * MODES]), near_copies, halo_copies

    def finish_image(halos, sides_out, factors, halo_copies):
        for copy in halo_copies:
            copy.wait_recv()
        for side in range(4):
            local[:, part(side)] = sides_out[side] + halos[side]
        project_pair(image, image_proj, factors, local)

    def eliminate(value):
        square[...] = value
        lane = lax.broadcasted_iota(jnp.int32, (COLS, 2 * COLS), 1)
        row = lax.broadcasted_iota(jnp.int32, (COLS, 2 * COLS), 0)

        def step(k, carry):
            table = square[...]
            line = square[pl.ds(k, 1), :]
            column = jnp.sum(jnp.where(lane == k, table, 0.0), axis=1, keepdims=True)
            pivot = jnp.sum(jnp.where(lane[0:1] == k, line, 0.0), axis=1, keepdims=True)
            line = line / pivot
            square[...] = jnp.where(row == k, line, table - column * line)
            return carry

        lax.fori_loop(0, COLS, step, 0)
        return square[:, COLS:]

    start_gram = 0.5 * exact(dirs[...], dirs[...], NT)
    energy, own_part, near_copies, halo_copies = dual(
        proj, halo_one, out_one, near_one, far_one, all_one
    )
    reduction = reduce_all(sum_a, jnp.concatenate([energy, start_gram], axis=1))
    next(reduction)
    for copy in near_copies:
        copy.wait_recv()
    arrived = gather_start(all_one, own_part + near_one[0] + near_one[1])
    next(reduction)
    crossed = gather_finish(all_one, arrived)
    next(reduction)
    crossed.wait_recv()
    finish_image(halo_one, far_one, coefficients(all_one), halo_copies)
    norm = 0.5 * exact(image[...], image[...], NT)
    next(reduction)
    second = reduce_all(sum_b, fold(norm))
    next(second)
    next(reduction)
    next(second)
    both_grams = next(reduction)
    curvature, descent = both_grams[:, :COLS], both_grams[:, COLS:]
    row = lax.broadcasted_iota(jnp.int32, (COLS, COLS), 0)
    lane = lax.broadcasted_iota(jnp.int32, (COLS, COLS), 1)
    identity = jnp.where(row == lane, 1.0, 0.0)
    inverse = eliminate(jnp.concatenate([curvature, identity], axis=1))
    step_t = exact(descent, inverse)
    next(second)
    next(second)
    next(second)
    norm = unfold(next(second))
    blend = exact(exact(step_t, norm), inverse)

    for side in range(4):
        at = part(side)
        start, moved = dirs[:, at], exact(step_t, image[:, at])
        resid[:, at] = start - moved
        first[:, at] = exact(step_t, start)
        dirs[:, at] = exact(blend, start) - moved
        proj[:, at] = exact(blend, proj[:, at]) - exact(step_t, image_proj[:, at])

    start_gram = 0.5 * exact(dirs[...], resid[...], NT)
    energy, own_part, near_copies, halo_copies = dual(
        proj, halo_two, out_two, near_two, far_two, all_two
    )
    reduction = reduce_all(sum_c, jnp.concatenate([energy, start_gram], axis=1))
    next(reduction)
    for copy in near_copies:
        copy.wait_recv()
    arrived = gather_start(all_two, own_part + near_two[0] + near_two[1])
    next(reduction)
    crossed = gather_finish(all_two, arrived)
    next(reduction)
    crossed.wait_recv()
    finish_image(halo_two, far_two, coefficients(all_two), halo_copies)
    next(reduction)
    next(reduction)
    step_t = eliminate(next(reduction)).T

    for side in range(4):
        at = part(side)
        rows = slice(side * FACE, (side + 1) * FACE)
        result = resid[:, at] - exact(step_t, image[:, at])
        out_res[rows, :] = result.T[:FACE]
        result = first[:, at] + exact(step_t, dirs[:, at])
        out_sol[rows, :] = result.T[:FACE]
    stores = [
        pltpu.make_async_copy(out_sol, sol_hbm.at[0, 0], local_sem.at[4]),
        pltpu.make_async_copy(out_res, res_hbm.at[0, 0], local_sem.at[5]),
    ]
    for store in stores:
        store.start()
    for wait in pending:
        wait()
    for store in stores:
        store.wait()


def shards(*arguments):
    def vmem(*shape, dtype=F32):
        return pltpu.VMEM(shape, dtype)

    def sums(rows):
        return (
            vmem(2, 2, rows, 128), vmem(4, rows, 128), vmem(4, rows, 128),
            vmem(8, rows, 128), vmem(2, rows, 128),
        )

    vector = vmem(COLS, WIDE)
    moments = vmem(2, 8, 16, 128)
    anywhere = pl.BlockSpec(memory_space=pl.ANY)
    out = jax.ShapeDtypeStruct((1, 1, ROWS, COLS), F32)
    return tuple(
        pl.pallas_call(
            kernel,
            out_shape=(out, out),
            in_specs=[
                anywhere, anywhere, pl.BlockSpec(memory_space=pltpu.SMEM),
                pl.BlockSpec(memory_space=pltpu.VMEM), anywhere, anywhere,
            ],
            out_specs=(anywhere, anywhere),
            scratch_shapes=[
                vmem(ROWS, ROWS), vmem(ROWS, ROWS, dtype=BF16), vmem(ROWS, ROWS, dtype=BF16),
                vmem(WIDE, ROWS, dtype=BF16), vmem(ROWS, WIDE, dtype=BF16),
                vmem(ROWS, COLS), vmem(4, FACE, COLS), vmem(MODES, 2 * FACE),
                vmem(2, MODES, 2 * FACE), vmem(COARSE + 3 * MODES, COARSE),
                vmem(4 * MODES, PAIR),
                vmem(8, WIDE), vector, vector, vector, vector, vector, vector, vector,
                vmem(4, COLS, SIDE), vmem(4, COLS, SIDE), vmem(2, 16, 128), vmem(2, 16, 128),
                vmem(2, 16, 128), vmem(2, 16, 128), vmem(4, COLS, SIDE), vmem(4, COLS, SIDE),
                moments, vmem(2, 8, MODES, 128), moments, moments,
                vmem(COARSE, 256), vmem(256, 256), vmem(256, 256), vmem(COARSE, COARSE + 256),
                sums(32), sums(16), sums(32), vmem(COLS, 128), vmem(ROWS, COLS), vmem(ROWS, COLS),
                pltpu.SemaphoreType.DMA((6,)), pltpu.SemaphoreType.DMA((64,)),
                pltpu.SemaphoreType.DMA((64,)),
            ],
            compiler_params=pltpu.CompilerParams(
                collective_id=0, has_side_effects=True, vmem_limit_bytes=60 * 1024 * 1024
            ),
        )(*arguments)
    )


def solution(mesh):
    return jax.shard_map(
        shards,
        mesh=mesh,
        in_specs=(
            P("cluster", "sub", None, None),
            P("cluster", "sub", None, None),
            P("cluster", "sub", None),
            P("cluster", "sub", None),
            P("cluster", "sub", None, None),
            P("cluster", None, None),
        ),
        out_specs=(P("cluster", "sub", None, None), P("cluster", "sub", None, None)),
        check_vma=False,
    )
```

time: 492 us -> 106 us (0.22)
  blocking collectives: 326 us -> 0 us
  Pallas kernels: 0 us -> 99 us
  starting transfers between devices: 52 us -> 0 us
  matrix products: 35.9 us -> 0 us
  other arithmetic: 33.3 us -> 0 us
  waiting for transfers between devices: 22.5 us -> 0 us
  local copies, waits for them, and re-layouts: 19.4 us -> 6.32 us
    psum x3 -> x0, blocking collectives: 236 us -> none  [the longest x2 163 us: shards(): lax.psum((0.5 * products(direction, mapped), 0.5 * products(direction, re...]
    pallas_call x0 -> x1, Pallas kernels: none -> 99 us  [shards(): pl.pallas_call(kernel, out_shape=(out, out), in_specs=[anywhere, anywhere...]
    all_gather x5 -> x0, blocking collectives: 89.7 us -> none  [project(): lax.all_gather(moments, 'sub', axis=0, tiled=True)]
    ppermute x22 -> x0, starting transfers between devices: 52 us -> none  [the longest x11 28.8 us: extended(): before = lax.ppermute(last, axis, up)]
    dot_general x27 -> x0, matrix products: 34.7 us -> none  [the longest x17 29.5 us: matmul(): jnp.dot(left, right, precision=precise, preferred_element_type=jnp.float32)]
    another operation x15 -> x0, other arithmetic: 24.2 us -> none  [the longest x6 13 us: shards(): factor = jnp.linalg.cholesky(curvature)]
    ppermute x22 -> x0, waiting for transfers between devices: 22.5 us -> none  [the longest x11 22.5 us: extended(): after = lax.ppermute(leading, axis, down)]
    gather x6 -> x0, local copies, waits for them, and re-layouts: 14.3 us -> none  [the longest x4 7.94 us: shards(): mapped = project(assemble(jnp.take(mapped, inverse_map, axis=0)))]
  transfers between devices with their start and end apart: 22 -> 0, of which waited for: 9 -> 0; matrix products, arithmetic and copies ran while one was open for 1% -> 0% of each run, Pallas kernels for 0% -> 0%
where the time goes in v1:
time: 106 us
  Pallas kernels  99 us (93%)
  local copies, waits for them, and re-layouts  6.32 us (6%)
    pallas_call x1, Pallas kernels, shards(): pl.pallas_call(kernel, out_shape=(out, out), in_specs=[anywhere, anywhere...  99 us
    pallas_call x2, local copies, waits for them, and re-layouts, shards(): pl.pallas_call(kernel, out_shape=(out, out), in_specs=[anywhere, anywhere...  4.19 us
    unnamed x1, local copies, waits for them, and re-layouts  2.12 us

profile of v1, /device:TPU:1, one launch (start us, length us, event | category | flops | bytes accessed | tf_op | source)
XLA Modules:
  0.0 106.0 jit_solution(14740264720977548693)
XLA Ops:
  0.6 2.1 %copy.8.contrib_hbm = f32[1,1,1408,64]{3,2,1,0:T(8,128)} copy(f32[1,1,1408,64]{2,3,1,0:T(8,128)} %param.7) | data formatting | bytes 720896 | tf_op args[1]
  2.8 99.0 %shard_map.77 = (f32[1,1,1408,64]{3,2,1,0:T(8,128)}, f32[1,1,1408,64]{3,2,1,0:T(8,128)}) custom-call(f32[1,1,1408,1408]{3,2,1,0:T(8,128)} %ops_hbm.1, f32[1,1,1408,64]{3,2,1,0:T(8,128)} %copy.8.contrib_hbm, s32[1,1,4]{2,1,0:T(1,128)} %sizes.1, s32[1,1,1408]{2,1,0:T(1,128)} %map_ref.1, f32[1,1,32,704]{3,2,1,0:T(8,128)} %basis_hbm.1, f32[1,512,512]{2,1,0:T(8,128)} %coarse_hbm.1), custom_call_target="tpu_custom_call" | custom-call | tf_op jit(solution)/shard_map/pallas_call | solution.py:447
  101.8 2.1 %copy.9 = f32[1,1,1408,64]{2,3,1,0:T(8,128)} copy(f32[1,1,1408,64]{3,2,1,0:T(8,128)} %get-tuple-element.2) | data formatting | bytes 720896 | tf_op jit(solution)/shard_map/pallas_call | solution.py:447
  103.9 2.1 %copy.10 = f32[1,1,1408,64]{2,3,1,0:T(8,128)} copy(f32[1,1,1408,64]{3,2,1,0:T(8,128)} %get-tuple-element.3) | data formatting | bytes 720896 | tf_op jit(solution)/shard_map/pallas_call | solution.py:447

commit v2 on v1

v2 whole, which is shorter than its diff:
```python
import jax
import jax.numpy as jnp
from jax import lax
from jax.sharding import PartitionSpec as P
from jax.experimental import pallas as pl
from jax.experimental.pallas import tpu as pltpu


ROWS = 1408
FACE = 352
SIDE = 384
WIDE = 4 * SIDE
PAIR = 2 * SIDE
COLS = 64
MODES = 32
SUBS = 16
COARSE = 512
SIGNS = (-1.0, 1.0, -1.0, 1.0)
WINDOWS = ((0, 384), (256, 512), (640, 512), (1024, 384))
FACING = (1, 0, 3, 2)

F32 = jnp.float32
BF16 = jnp.bfloat16
NN = (((1,), (0,)), ((), ()))
NT = (((1,), (1,)), ((), ()))


def exact(left, right, dims=NN):
    return lax.dot_general(
        left, right, dims, precision=lax.Precision.HIGHEST, preferred_element_type=F32
    )


def single(left, right):
    return lax.dot_general(left, right, NN, preferred_element_type=F32)


def split(value):
    high = value.astype(BF16)
    return high, (value - high.astype(F32)).astype(BF16)


def fold(value):
    half = value.shape[0] // 2
    return jnp.concatenate([value[:half], value[half:]], axis=1)


def unfold(value):
    half = value.shape[1] // 2
    return jnp.concatenate([value[:, :half], value[:, half:]], axis=0)


def part(side):
    return slice(side * SIDE, (side + 1) * SIDE)


def eliminate(left, right):
    joined = jnp.concatenate([left, right], axis=1)
    table = [joined[8 * r : 8 * r + 8] for r in range(8)]
    row = lax.broadcasted_iota(jnp.int32, (8, 2 * COLS), 0)
    for block in range(8):
        columns = [
            [
                jnp.broadcast_to(rows[:, 8 * block + j : 8 * block + j + 1], (8, 2 * COLS))
                for j in range(8)
            ]
            for rows in table
        ]
        panel, own = table[block], columns[block]
        for j in range(8):
            scale = 1.0 / own[j][j : j + 1]
            line = panel[j : j + 1] * scale
            panel = jnp.where(row == j, line, panel - own[j] * line)
            for k in range(j + 1, 8):
                entry = own[k][j : j + 1] * scale
                own[k] = jnp.where(row == j, entry, own[k] - own[j] * entry)
        for r in range(8):
            if r == block:
                table[r] = panel
            else:
                for j in range(8):
                    table[r] = table[r] - columns[r][j] * panel[j : j + 1]
    return jnp.concatenate(table, axis=0)[:, COLS:]


def kernel(
    ops_hbm, contrib_hbm, sizes, map_ref, basis_hbm, coarse_hbm,
    sol_hbm, res_hbm,
    full, high, low, scatter, gather, moments_slots,
    own_rhs, halo_rhs, own_basis, near_basis, coarse, moments_map,
    weights, first, basis, proj, image_proj, local,
    halo_one, halo_two, near_one, near_two, out_one, out_two, far_one, far_two,
    all_q, all_m, all_one, all_two, mixed, table_even, table_odd, dense_m,
    sum_a, sum_b, sum_c, out_sol, out_res,
    local_sem, send_sem, recv_sem,
):
    c, s = lax.axis_index("cluster"), lax.axis_index("sub")
    x, y = lax.div(c, 4), lax.rem(c, 4)
    z, core = lax.div(s, 2), lax.rem(s, 2)
    down, up = lax.rem(s + SUBS - 1, SUBS), lax.rem(s + 1, SUBS)
    west, east = lax.rem(c + 15, 16), lax.rem(c + 1, 16)
    mate = z * 2 + 1 - core
    x_peers = [(lax.rem(x + i, 4) * 4 + y, s) for i in range(1, 4)]
    y_peers = [(x * 4 + lax.rem(y + i, 4), s) for i in range(1, 4)]
    z_peers = [(c, lax.rem(z + i, 8) * 2 + core) for i in range(1, 8)]
    side_peers = ((c, down), (c, up), (west, s), (east, s))
    used = [0]

    def fresh():
        used[0] += 1
        return used[0] - 1

    loads = [
        pltpu.make_async_copy(contrib_hbm.at[0, 0], own_rhs, local_sem.at[0]),
        pltpu.make_async_copy(basis_hbm.at[0, 0], own_basis, local_sem.at[1]),
        pltpu.make_async_copy(
            coarse_hbm.at[0], coarse.at[pl.ds(MODES, COARSE)], local_sem.at[2]
        ),
        pltpu.make_async_copy(ops_hbm.at[0, 0], full, local_sem.at[3]),
    ]
    for load in loads:
        load.start()

    barrier = pltpu.get_barrier_semaphore()
    greeted = [(c, mate)] + z_peers + x_peers + y_peers
    greeted += [(c, down), (c, up), (west, s), (east, s)]
    for peer in greeted:
        pl.semaphore_signal(
            barrier, inc=1, device_id=peer, device_id_type=pl.DeviceIdType.MESH
        )
    pl.semaphore_wait(barrier, len(greeted))

    def send(source, target, peer, slot):
        copy = pltpu.make_async_remote_copy(
            src_ref=source, dst_ref=target,
            send_sem=send_sem.at[slot], recv_sem=recv_sem.at[slot],
            device_id=peer, device_id_type=pl.DeviceIdType.MESH,
        )
        copy.start()
        return copy

    pending = []

    def share(buffer, me, peers):
        slot = fresh()
        for peer in peers:
            send(buffer.at[me], buffer.at[me], peer, slot)
        whole = buffer.at[pl.ds(0, len(peers))]
        pending.append(lambda: pltpu.make_async_copy(whole, whole, send_sem.at[slot]).wait())
        return pltpu.make_async_copy(whole, whole, recv_sem.at[slot])

    def swap(source, target, peer):
        copy = send(source, target, peer, fresh())
        pending.append(copy.wait_send)
        return copy

    rhs_copies = []
    for side in range(4):
        start, length = WINDOWS[side]
        rhs_copies.append(
            swap(
                contrib_hbm.at[0, 0, :, pl.ds(start, length)],
                halo_rhs.at[FACING[side], :, pl.ds(0, length)],
                side_peers[side],
            )
        )
    basis_copies = [
        swap(basis_hbm.at[0, 0], near_basis.at[1], (c, down)),
        swap(basis_hbm.at[0, 0], near_basis.at[0], (c, up)),
    ]

    slots = map_ref[0]
    slots = slots + (SIDE - FACE) * (
        (slots >= FACE).astype(jnp.int32)
        + (slots >= 2 * FACE).astype(jnp.int32)
        + (slots >= 3 * FACE).astype(jnp.int32)
    )

    def fill_scatter(step, carry):
        rows = pl.ds(pl.multiple_of(step * 128, 128), 128)
        index = lax.broadcasted_iota(jnp.int32, (128, ROWS), 0) + step * 128
        scatter[rows, :] = jnp.where(index == slots, 1.0, 0.0).astype(BF16)
        return carry

    lax.fori_loop(0, WIDE // 128, fill_scatter, 0)
    lanes = lax.broadcasted_iota(jnp.int32, (8, SIDE), 1)
    for side in range(4):
        weights[:, part(side)] = jnp.where(lanes < sizes[0, 0, side], SIGNS[side], 0.0)

    loads[1].wait()
    zero_lanes = jnp.zeros((MODES, SIDE - FACE), F32)

    def half_basis(value, side):
        return jnp.concatenate(
            [value[:, side * FACE : (side + 1) * FACE], zero_lanes], axis=1
        )

    weight_low, weight_high = weights[0:1, part(0)], weights[0:1, part(1)]
    empty = jnp.zeros((MODES, SIDE), F32)
    mine = own_basis[...]
    moments_map[MODES : 2 * MODES, part(0)] = half_basis(mine, 0) * weight_low
    moments_map[MODES : 2 * MODES, part(1)] = half_basis(mine, 1) * weight_high
    for copy in basis_copies:
        copy.wait_recv()
    moments_map[0:MODES, part(0)] = -half_basis(near_basis[0], 1) * weight_low
    moments_map[0:MODES, part(1)] = empty
    moments_map[2 * MODES : 3 * MODES, part(0)] = empty
    moments_map[2 * MODES : 3 * MODES, part(1)] = (
        -half_basis(near_basis[1], 0) * weight_high
    )
    moments_map[3 * MODES : 4 * MODES, :] = jnp.zeros((MODES, PAIR), F32)

    def gather_start(buffer, value):
        buffer[core, z] = value
        return share(buffer.at[core], z, z_peers)

    def gather_finish(buffer, arrived):
        arrived.wait()
        return swap(buffer.at[core], buffer.at[core], (c, mate))

    loads[0].wait()
    for copy in rhs_copies:
        copy.wait_recv()
    index = lax.broadcasted_iota(jnp.int32, (COLS, FACE), 1)
    zero_columns = jnp.zeros((COLS, SIDE - FACE), F32)
    for side in range(4):
        shift = FACING[side] * FACE - WINDOWS[FACING[side]][0]
        own = own_rhs[:, side * FACE : (side + 1) * FACE]
        other = halo_rhs[side][:, shift : shift + FACE]
        joined = jnp.where(index < sizes[0, 0, side], SIGNS[side] * (own - other), 0.0)
        first[:, part(side)] = jnp.concatenate([joined, zero_columns], axis=1)
    q_moments = exact(moments_map[MODES : 2 * MODES, :], first[:, :PAIR], NT)
    q_arrived = gather_start(all_q, fold(q_moments))
    m_own = exact(moments_map[MODES : 2 * MODES, :], moments_map[...], NT)
    m_own = jnp.concatenate(
        [0.5 * m_own[:, MODES : 2 * MODES], m_own[:, 2 * MODES : 3 * MODES]], axis=1
    )
    m_arrived = gather_start(all_m, fold(m_own))

    columns = lax.broadcasted_iota(jnp.int32, (128, 128), 1).astype(F32)
    for step in range(ROWS // 128):
        piece = slots[:, step * 128 : (step + 1) * 128].astype(F32)
        tall = jnp.broadcast_to(piece, (128, 128)).T
        for tile in range(WIDE // 128):
            gather[step * 128 : (step + 1) * 128, tile * 128 : (tile + 1) * 128] = (
                jnp.where(tall == columns + float(tile * 128), 1.0, 0.0).astype(BF16)
            )

    def split_rows(step, carry):
        rows = pl.ds(pl.multiple_of(step * 64, 64), 64)
        high[rows, :], low[rows, :] = split(full[rows, :])
        return carry

    map_high, map_low = split(moments_map[...] * weights[0:1, :PAIR])
    spread = single(jnp.concatenate([map_high, map_low], axis=0), scatter[:PAIR, :])
    map_high, map_low = split(spread[: 4 * MODES] + spread[4 * MODES :])
    moments_slots[: 4 * MODES] = map_high
    moments_slots[4 * MODES :] = map_low

    loads[2].wait()
    coarse[0:MODES, :] = jnp.zeros((MODES, COARSE), F32)
    coarse[MODES + COARSE :, :] = jnp.zeros((2 * MODES, COARSE), F32)
    near_rows = coarse[pl.ds(pl.multiple_of(s * MODES, MODES), 4 * MODES), :]
    near = near_rows.T
    dense_m[...] = jnp.zeros((COARSE, COARSE + 128), F32)

    q_crossed = gather_finish(all_q, q_arrived)
    m_crossed = gather_finish(all_m, m_arrived)
    loads[3].wait()
    lax.fori_loop(0, ROWS // 64, split_rows, 0)
    m_crossed.wait_recv()
    lane = lax.broadcasted_iota(jnp.int32, (MODES, 128), 1)
    blank = jnp.zeros((MODES, 64), F32)
    for block in range(SUBS):
        tile, shift = block // 4, 32 * (block % 4)
        rows = slice(block * MODES, (block + 1) * MODES)
        value = jnp.concatenate([unfold(all_m[block % 2, block // 2]), blank], axis=1)
        if shift:
            value = pltpu.roll(value, shift, 1)
        if shift == 96:
            dense_m[rows, (tile + 1) * 128 : (tile + 2) * 128] = jnp.where(
                lane < shift, value, 0.0
            )
            value = jnp.where(lane >= shift, value, 0.0)
        dense_m[rows, tile * 128 : (tile + 1) * 128] = value
    square_m = dense_m[:, :COARSE]
    square_m = square_m + square_m.T
    inner = coarse[MODES : MODES + COARSE, :]
    mixed[:, 0:128] = near
    mixed[:, 128:256] = near - exact(inner, exact(square_m, near))
    for block in range(SUBS):
        to = ((block % 2) * 8 + block // 2) * 16
        table_even[to : to + 16, :] = mixed[block * MODES : block * MODES + 16, :]
        table_odd[to : to + 16, :] = mixed[block * MODES + 16 : (block + 1) * MODES, :]

    def coefficients(buffer):
        turned = buffer[...].reshape(SUBS * 16, 128).T
        return exact(turned[:COLS], table_even[...]) + exact(
            turned[COLS:], table_odd[...]
        )

    def place(which):
        return slice(which * COLS, (which + 1) * COLS)

    def project_pair(which, value_proj, factors, source):
        lift = exact(
            jnp.concatenate([factors[:, :128], factors[:, 128:]], axis=0),
            moments_map[...],
        )
        once = source[:, :PAIR] - lift[:COLS]
        basis[place(which), :PAIR] = once
        value_proj[:, :PAIR] = once - lift[COLS:]
        basis[place(which), PAIR:] = source[:, PAIR:]
        value_proj[:, PAIR:] = source[:, PAIR:]

    q_crossed.wait_recv()
    project_pair(0, proj, coefficients(all_q), first)

    def reduce_all(bufs, value):
        mates, along_x, along_y, along_z, halves = bufs
        rows = value.shape[0] // 2
        mates[core, 0] = value[:rows]
        mates[core, 1] = value[rows:]
        copy = swap(mates.at[core, 1 - core], mates.at[core, 1 - core], (c, mate))
        yield
        copy.wait_recv()
        along_x[x] = mates[0, core] + mates[1, core]
        arrived = share(along_x, x, x_peers)
        yield
        arrived.wait()
        along_y[y] = (along_x[0] + along_x[1]) + (along_x[2] + along_x[3])
        arrived = share(along_y, y, y_peers)
        yield
        arrived.wait()
        along_z[z] = (along_y[0] + along_y[1]) + (along_y[2] + along_y[3])
        arrived = share(along_z, z, z_peers)
        yield
        arrived.wait()
        total = along_z[0]
        for i in range(1, 8):
            total = total + along_z[i]
        halves[core] = total
        copy = swap(halves.at[core], halves.at[core], (c, mate))
        yield
        copy.wait_recv()
        yield jnp.concatenate([halves[0], halves[1]], axis=0)

    def three_parts(value):
        high_v = value.astype(BF16)
        rest = value - high_v.astype(F32)
        return jnp.concatenate((high_v,) + split(rest), axis=0)

    def spread_slots(source):
        return single(three_parts(source[...] * weights[0:1, :]), scatter[...]).astype(BF16)

    def product(both):
        turned, small = single(both, high[...]), single(both[: 2 * COLS], low[...])
        return turned[:COLS] + (
            (turned[COLS : 2 * COLS] + small[:COLS])
            + (turned[2 * COLS :] + small[COLS:])
        )

    def energy(both, value):
        whole = both.astype(F32)
        whole = whole[:COLS] + (whole[COLS : 2 * COLS] + whole[2 * COLS :])
        return exact(whole, value, NT)

    def send_moments(parts, outs, nears):
        both = lax.dot_general(
            moments_slots[...], parts[: 2 * COLS], NT, preferred_element_type=F32
        )
        half = 4 * MODES
        shares = both[:half, :COLS] + both[half:, :COLS] + both[:half, COLS:]
        outs[0] = fold(shares[0:MODES])
        outs[1] = fold(shares[2 * MODES : 3 * MODES])
        copies = [
            swap(outs.at[0], nears.at[1], (c, down)),
            swap(outs.at[1], nears.at[0], (c, up)),
        ]
        return fold(shares[MODES : 2 * MODES]), copies

    def send_sides(parts, halos, sides_out):
        back = single(parts, gather[...])
        back = back[:COLS] + (back[COLS : 2 * COLS] + back[2 * COLS :])
        back = back * weights[0:1, :]
        copies = []
        for side in (2, 3, 0, 1):
            sides_out[side] = back[:, part(side)]
            copies.append(
                swap(sides_out.at[side], halos.at[FACING[side]], side_peers[side])
            )
        return copies

    def both_parts(value):
        return jnp.concatenate(split(value), axis=0)

    def join_sides(halos, sides_out, copies):
        for copy in copies:
            copy.wait_recv()
        for side in range(4):
            local[:, part(side)] = sides_out[side] + halos[side]

    spread = spread_slots(proj)
    value = product(spread)
    parts = three_parts(value)
    own_part, near_copies = send_moments(parts, out_one, near_one)
    halo_copies = send_sides(parts, halo_one, far_one)
    curvature = energy(spread, value)
    start = basis[place(0), :]
    descent = 0.5 * exact(start, start, NT)
    reduction = reduce_all(sum_a, jnp.concatenate([curvature, descent], axis=1))
    next(reduction)
    for copy in near_copies:
        copy.wait_recv()
    arrived = gather_start(all_one, own_part + near_one[0] + near_one[1])
    next(reduction)
    join_sides(halo_one, far_one, halo_copies)
    next(reduction)
    crossed = gather_finish(all_one, arrived)
    next(reduction)
    crossed.wait_recv()
    project_pair(1, image_proj, coefficients(all_one), local)
    image = basis[place(1), :]
    second = reduce_all(sum_b, fold(0.5 * exact(image, image, NT)))
    next(second)

    spread = spread_slots(image_proj)
    next(second)
    value = product(spread)
    third = reduce_all(sum_c, fold(energy(spread, value)))
    next(third)
    next(second)
    next(reduction)
    parts = three_parts(value)
    own_part, near_copies = send_moments(parts, out_two, near_two)
    next(third)
    halo_copies = send_sides(parts, halo_two, far_two)
    both_grams = next(reduction)
    curvature, descent = both_grams[:, :COLS], both_grams[:, COLS:]
    next(second)
    row = lax.broadcasted_iota(jnp.int32, (COLS, COLS), 0)
    lane = lax.broadcasted_iota(jnp.int32, (COLS, COLS), 1)
    inverse = eliminate(curvature, jnp.where(row == lane, 1.0, 0.0))
    next(third)
    for copy in near_copies:
        copy.wait_recv()
    arrived = gather_start(all_two, own_part + near_two[0] + near_two[1])
    alpha, alpha_t = exact(inverse, descent), exact(descent, inverse)
    next(second)
    next(third)
    norm = unfold(next(second))
    moved = exact(norm, alpha)
    blend = exact(inverse, moved)
    known = exact(alpha_t, exact(norm, blend))
    descent_two = exact(alpha_t, moved) - descent
    crossed = gather_finish(all_two, arrived)
    join_sides(halo_two, far_two, halo_copies)
    crossed.wait_recv()
    factors = coefficients(all_two)
    lift = exact(factors[:, :128], moments_map[...])
    basis[place(2), :PAIR] = local[:, :PAIR] - lift
    basis[place(2), PAIR:] = local[:, PAIR:]
    next(third)
    cubic = unfold(next(third))

    curvature_two = exact(alpha_t, exact(cubic, alpha)) - known
    alpha_two = eliminate(curvature_two, descent_two)
    outer = (alpha + exact(blend, alpha_two)).T
    cross = exact(alpha, alpha_two).T
    none = jnp.zeros((COLS, COLS), F32)
    mix = jnp.concatenate(
        [
            jnp.concatenate([outer, -cross, none], axis=1),
            jnp.concatenate([none, -outer, cross], axis=1),
        ],
        axis=0,
    )
    for side in range(4):
        result = exact(mix, basis[:, part(side)])
        at = slice(side * FACE, (side + 1) * FACE)
        out_sol[:, at] = result[:COLS, :FACE]
        out_res[:, at] = (basis[place(0), part(side)] + result[COLS:])[:, :FACE]
    stores = [
        pltpu.make_async_copy(out_sol, sol_hbm.at[0, 0], local_sem.at[4]),
        pltpu.make_async_copy(out_res, res_hbm.at[0, 0], local_sem.at[5]),
    ]
    for store in stores:
        store.start()
    for wait in pending:
        wait()
    for store in stores:
        store.wait()


def shards(dual_ops, contributions, block_sizes, mult_map, coarse_basis, coarse_inverse):
    def vmem(*shape, dtype=F32):
        return pltpu.VMEM(shape, dtype)

    def sums(rows):
        return (
            vmem(2, 2, rows, 128), vmem(4, rows, 128), vmem(4, rows, 128),
            vmem(8, rows, 128), vmem(2, rows, 128),
        )

    vector = vmem(COLS, WIDE)
    moments = vmem(2, 8, 16, 128)
    sides, pair = vmem(4, COLS, SIDE), vmem(2, 16, 128)
    anywhere = pl.BlockSpec(memory_space=pl.ANY)
    out = jax.ShapeDtypeStruct((1, 1, COLS, ROWS), F32)
    results = pl.pallas_call(
        kernel,
        out_shape=(out, out),
        in_specs=[
            anywhere, anywhere, pl.BlockSpec(memory_space=pltpu.SMEM),
            pl.BlockSpec(memory_space=pltpu.VMEM), anywhere, anywhere,
        ],
        out_specs=(anywhere, anywhere),
        scratch_shapes=[
            vmem(ROWS, ROWS), vmem(ROWS, ROWS, dtype=BF16), vmem(ROWS, ROWS, dtype=BF16),
            vmem(WIDE, ROWS, dtype=BF16), vmem(ROWS, WIDE, dtype=BF16),
            vmem(8 * MODES, ROWS, dtype=BF16),
            vmem(COLS, ROWS), vmem(4, COLS, 512), vmem(MODES, 2 * FACE),
            vmem(2, MODES, 2 * FACE), vmem(COARSE + 3 * MODES, COARSE),
            vmem(4 * MODES, PAIR),
            vmem(8, WIDE), vector, vmem(3 * COLS, WIDE), vector, vector, vector,
            sides, sides, pair, pair, pair, pair, sides, sides,
            moments, moments, moments, moments,
            vmem(COARSE, 256), vmem(256, 256), vmem(256, 256), vmem(COARSE, COARSE + 128),
            sums(32), sums(16), sums(16), vmem(COLS, ROWS), vmem(COLS, ROWS),
            pltpu.SemaphoreType.DMA((6,)), pltpu.SemaphoreType.DMA((64,)),
            pltpu.SemaphoreType.DMA((64,)),
        ],
        compiler_params=pltpu.CompilerParams(
            collective_id=0, has_side_effects=True, vmem_limit_bytes=60 * 1024 * 1024
        ),
    )(
        dual_ops, jnp.swapaxes(contributions, 2, 3), block_sizes, mult_map,
        coarse_basis, coarse_inverse,
    )
    return tuple(jnp.swapaxes(result, 2, 3) for result in results)


def solution(mesh):
    return jax.shard_map(
        shards,
        mesh=mesh,
        in_specs=(
            P("cluster", "sub", None, None),
            P("cluster", "sub", None, None),
            P("cluster", "sub", None),
            P("cluster", "sub", None),
            P("cluster", "sub", None, None),
            P("cluster", None, None),
        ),
        out_specs=(P("cluster", "sub", None, None), P("cluster", "sub", None, None)),
        check_vma=False,
    )
```

time: 106 us -> 75.5 us (0.71)
  Pallas kernels: 99 us -> 71.2 us
  local copies, waits for them, and re-layouts: 6.32 us -> 3.48 us
    pallas_call x1, Pallas kernels: 99 us -> 71.2 us  [shards(): pl.pallas_call(kernel, out_shape=(out, out), in_specs=[anywhere, anywhere...]
    pallas_call x2 -> x0, local copies, waits for them, and re-layouts: 4.19 us -> none  [shards(): pl.pallas_call(kernel, out_shape=(out, out), in_specs=[anywhere, anywhere...]
    unnamed x1 -> x2, local copies, waits for them, and re-layouts: 2.12 us -> 3.48 us
where the time goes in v2:
time: 75.5 us; the launch traced here: 75.3 us
  Pallas kernels  71.2 us (94%)
  local copies, waits for them, and re-layouts  3.48 us (5%)
    pallas_call x1, Pallas kernels, shards(): pl.pallas_call(kernel, out_shape=(out, out), in_specs=[anywhere, anywhere...  71.2 us
    unnamed x2, local copies, waits for them, and re-layouts  3.48 us

profile of v2, /device:TPU:1, one launch (start us, length us, event | category | flops | bytes accessed | tf_op | source)
XLA Modules:
  0.0 75.3 jit_solution(15372269127326021428)
XLA Ops:
  0.6 71.2 %shard_map.77 = (f32[1,1,64,1408]{3,2,1,0:T(8,128)}, f32[1,1,64,1408]{3,2,1,0:T(8,128)}) custom-call(f32[1,1,1408,1408]{3,2,1,0:T(8,128)} %ops_hbm.1, f32[1,1,64,1408]{3,2,1,0:T(8,128)} %bitcast.3, s32[1,1,4]{2,1,0:T(1,128)} %sizes.1, s32[1,1,1408]{2,1,0:T(1,128)} %map_ref.1, f32[1,1,32,704]{3,2,1,0:T(8,128)} %basis_hbm.1, f32[1,512,512]{2,1,0:T(8,128)} %coarse_hbm.1), custom_call_target="tpu_custom_call" | custom-call | tf_op jit(solution)/shard_map/pallas_call | solution.py:510
  71.8 1.7 %copy.10 = f32[1,1,1408,64]{2,3,1,0:T(8,128)} copy(f32[1,1,1408,64]{2,3,1,0:T(8,128)} %bitcast.5) | data formatting | bytes 720896
  73.6 1.7 %copy.11 = f32[1,1,1408,64]{2,3,1,0:T(8,128)} copy(f32[1,1,1408,64]{2,3,1,0:T(8,128)} %bitcast.4) | data formatting | bytes 720896

commit v3 on v2

--- a/solution.py
+++ b/solution.py
@@ -16,7 +16,6 @@
 SUBS = 16
 COARSE = 512
 SIGNS = (-1.0, 1.0, -1.0, 1.0)
-WINDOWS = ((0, 384), (256, 512), (640, 512), (1024, 384))
 FACING = (1, 0, 3, 2)
 
 F32 = jnp.float32
@@ -87,7 +86,7 @@
     ops_hbm, contrib_hbm, sizes, map_ref, basis_hbm, coarse_hbm,
     sol_hbm, res_hbm,
     full, high, low, scatter, gather, moments_slots,
-    own_rhs, halo_rhs, own_basis, near_basis, coarse, moments_map,
+    own_rhs, halo_q, far_q, own_basis, half_basis, near_basis, coarse, moments_map,
     weights, first, basis, proj, image_proj, local,
     halo_one, halo_two, near_one, near_two, out_one, out_two, far_one, far_two,
     all_q, all_m, all_one, all_two, mixed, table_even, table_odd, dense_m,
@@ -100,9 +99,10 @@
     down, up = lax.rem(s + SUBS - 1, SUBS), lax.rem(s + 1, SUBS)
     west, east = lax.rem(c + 15, 16), lax.rem(c + 1, 16)
     mate = z * 2 + 1 - core
-    x_peers = [(lax.rem(x + i, 4) * 4 + y, s) for i in range(1, 4)]
-    y_peers = [(x * 4 + lax.rem(y + i, 4), s) for i in range(1, 4)]
-    z_peers = [(c, lax.rem(z + i, 8) * 2 + core) for i in range(1, 8)]
+    x_peers = [(lax.rem(x + i, 4) * 4 + y, s) for i in (2, 1, 3)]
+    x_others = [(lax.rem(x + i, 4) * 4 + y, mate) for i in (2, 1, 3, 0)]
+    y_peers = [(x * 4 + lax.rem(y + i, 4), s) for i in (2, 1, 3)]
+    z_peers = [(c, lax.rem(z + i, 8) * 2 + core) for i in (4, 3, 5, 2, 6, 1, 7)]
     side_peers = ((c, down), (c, up), (west, s), (east, s))
     used = [0]
 
@@ -122,12 +122,28 @@
         load.start()
 
     barrier = pltpu.get_barrier_semaphore()
-    greeted = [(c, mate)] + z_peers + x_peers + y_peers
+    greeted = z_peers + x_peers + x_others + y_peers
     greeted += [(c, down), (c, up), (west, s), (east, s)]
     for peer in greeted:
         pl.semaphore_signal(
             barrier, inc=1, device_id=peer, device_id_type=pl.DeviceIdType.MESH
         )
+
+    lanes = lax.broadcasted_iota(jnp.int32, (8, SIDE), 1)
+    for side in range(4):
+        weights[:, part(side)] = jnp.where(lanes < sizes[0, 0, side], SIGNS[side], 0.0)
+    loads[0].wait()
+    zero_columns = jnp.zeros((COLS, SIDE - FACE), F32)
+    for side in range(4):
+        own = own_rhs[:, side * FACE : (side + 1) * FACE]
+        far_q[side] = (
+            jnp.concatenate([own, zero_columns], axis=1) * weights[0:1, part(side)]
+        )
+    loads[1].wait()
+    zero_lanes = jnp.zeros((MODES, SIDE - FACE), F32)
+    for side in range(2):
+        own = own_basis[:, side * FACE : (side + 1) * FACE]
+        half_basis[side] = jnp.concatenate([own, zero_lanes], axis=1)
     pl.semaphore_wait(barrier, len(greeted))
 
     def send(source, target, peer, slot):
@@ -154,19 +170,13 @@
         pending.append(copy.wait_send)
         return copy
 
-    rhs_copies = []
-    for side in range(4):
-        start, length = WINDOWS[side]
-        rhs_copies.append(
-            swap(
-                contrib_hbm.at[0, 0, :, pl.ds(start, length)],
-                halo_rhs.at[FACING[side], :, pl.ds(0, length)],
-                side_peers[side],
-            )
-        )
     basis_copies = [
-        swap(basis_hbm.at[0, 0], near_basis.at[1], (c, down)),
-        swap(basis_hbm.at[0, 0], near_basis.at[0], (c, up)),
+        swap(half_basis.at[0], near_basis.at[1], (c, down)),
+        swap(half_basis.at[1], near_basis.at[0], (c, up)),
+    ]
+    rhs_copies = [
+        swap(far_q.at[side], halo_q.at[FACING[side]], side_peers[side])
+        for side in (2, 3, 0, 1)
     ]
 
     slots = map_ref[0]
@@ -183,60 +193,6 @@
         return carry
 
     lax.fori_loop(0, WIDE // 128, fill_scatter, 0)
-    lanes = lax.broadcasted_iota(jnp.int32, (8, SIDE), 1)
-    for side in range(4):
-        weights[:, part(side)] = jnp.where(lanes < sizes[0, 0, side], SIGNS[side], 0.0)
-
-    loads[1].wait()
-    zero_lanes = jnp.zeros((MODES, SIDE - FACE), F32)
-
-    def half_basis(value, side):
-        return jnp.concatenate(
-            [value[:, side * FACE : (side + 1) * FACE], zero_lanes], axis=1
-        )
-
-    weight_low, weight_high = weights[0:1, part(0)], weights[0:1, part(1)]
-    empty = jnp.zeros((MODES, SIDE), F32)
-    mine = own_basis[...]
-    moments_map[MODES : 2 * MODES, part(0)] = half_basis(mine, 0) * weight_low
-    moments_map[MODES : 2 * MODES, part(1)] = half_basis(mine, 1) * weight_high
-    for copy in basis_copies:
-        copy.wait_recv()
-    moments_map[0:MODES, part(0)] = -half_basis(near_basis[0], 1) * weight_low
-    moments_map[0:MODES, part(1)] = empty
-    moments_map[2 * MODES : 3 * MODES, part(0)] = empty
-    moments_map[2 * MODES : 3 * MODES, part(1)] = (
-        -half_basis(near_basis[1], 0) * weight_high
-    )
-    moments_map[3 * MODES : 4 * MODES, :] = jnp.zeros((MODES, PAIR), F32)
-
-    def gather_start(buffer, value):
-        buffer[core, z] = value
-        return share(buffer.at[core], z, z_peers)
-
-    def gather_finish(buffer, arrived):
-        arrived.wait()
-        return swap(buffer.at[core], buffer.at[core], (c, mate))
-
-    loads[0].wait()
-    for copy in rhs_copies:
-        copy.wait_recv()
-    index = lax.broadcasted_iota(jnp.int32, (COLS, FACE), 1)
-    zero_columns = jnp.zeros((COLS, SIDE - FACE), F32)
-    for side in range(4):
-        shift = FACING[side] * FACE - WINDOWS[FACING[side]][0]
-        own = own_rhs[:, side * FACE : (side + 1) * FACE]
-        other = halo_rhs[side][:, shift : shift + FACE]
-        joined = jnp.where(index < sizes[0, 0, side], SIGNS[side] * (own - other), 0.0)
-        first[:, part(side)] = jnp.concatenate([joined, zero_columns], axis=1)
-    q_moments = exact(moments_map[MODES : 2 * MODES, :], first[:, :PAIR], NT)
-    q_arrived = gather_start(all_q, fold(q_moments))
-    m_own = exact(moments_map[MODES : 2 * MODES, :], moments_map[...], NT)
-    m_own = jnp.concatenate(
-        [0.5 * m_own[:, MODES : 2 * MODES], m_own[:, 2 * MODES : 3 * MODES]], axis=1
-    )
-    m_arrived = gather_start(all_m, fold(m_own))
-
     columns = lax.broadcasted_iota(jnp.int32, (128, 128), 1).astype(F32)
     for step in range(ROWS // 128):
         piece = slots[:, step * 128 : (step + 1) * 128].astype(F32)
@@ -246,10 +202,49 @@
                 jnp.where(tall == columns + float(tile * 128), 1.0, 0.0).astype(BF16)
             )
 
+    loads[3].wait()
+
     def split_rows(step, carry):
         rows = pl.ds(pl.multiple_of(step * 64, 64), 64)
         high[rows, :], low[rows, :] = split(full[rows, :])
         return carry
+
+    lax.fori_loop(0, ROWS // 64, split_rows, 0)
+
+    weight_low, weight_high = weights[0:1, part(0)], weights[0:1, part(1)]
+    empty = jnp.zeros((MODES, SIDE), F32)
+    moments_map[MODES : 2 * MODES, part(0)] = half_basis[0] * weight_low
+    moments_map[MODES : 2 * MODES, part(1)] = half_basis[1] * weight_high
+    for copy in basis_copies:
+        copy.wait_recv()
+    moments_map[0:MODES, part(0)] = -near_basis[0] * weight_low
+    moments_map[0:MODES, part(1)] = empty
+    moments_map[2 * MODES : 3 * MODES, part(0)] = empty
+    moments_map[2 * MODES : 3 * MODES, part(1)] = -near_basis[1] * weight_high
+    moments_map[3 * MODES : 4 * MODES, :] = jnp.zeros((MODES, PAIR), F32)
+
+    def gather_start(buffer, value):
+        buffer[core, z] = value
+        return share(buffer.at[core], z, z_peers)
+
+    def gather_finish(buffer, arrived):
+        arrived.wait()
+        return swap(buffer.at[core], buffer.at[core], (c, mate))
+
+    def join_sides(target, halos, sides_out, copies):
+        for copy in copies:
+            copy.wait_recv()
+        for side in range(4):
+            target[:, part(side)] = sides_out[side] + halos[side]
+
+    join_sides(first, halo_q, far_q, rhs_copies)
+    q_moments = exact(moments_map[MODES : 2 * MODES, :], first[:, :PAIR], NT)
+    q_arrived = gather_start(all_q, fold(q_moments))
+    m_own = exact(moments_map[MODES : 2 * MODES, :], moments_map[...], NT)
+    m_own = jnp.concatenate(
+        [0.5 * m_own[:, MODES : 2 * MODES], m_own[:, 2 * MODES : 3 * MODES]], axis=1
+    )
+    m_arrived = gather_start(all_m, fold(m_own))
 
     map_high, map_low = split(moments_map[...] * weights[0:1, :PAIR])
     spread = single(jnp.concatenate([map_high, map_low], axis=0), scatter[:PAIR, :])
@@ -261,13 +256,11 @@
     coarse[0:MODES, :] = jnp.zeros((MODES, COARSE), F32)
     coarse[MODES + COARSE :, :] = jnp.zeros((2 * MODES, COARSE), F32)
     near_rows = coarse[pl.ds(pl.multiple_of(s * MODES, MODES), 4 * MODES), :]
-    near = near_rows.T
+    mixed[:, 0:128] = near_rows.T
     dense_m[...] = jnp.zeros((COARSE, COARSE + 128), F32)
 
     q_crossed = gather_finish(all_q, q_arrived)
     m_crossed = gather_finish(all_m, m_arrived)
-    loads[3].wait()
-    lax.fori_loop(0, ROWS // 64, split_rows, 0)
     m_crossed.wait_recv()
     lane = lax.broadcasted_iota(jnp.int32, (MODES, 128), 1)
     blank = jnp.zeros((MODES, 64), F32)
@@ -286,8 +279,7 @@
     square_m = dense_m[:, :COARSE]
     square_m = square_m + square_m.T
     inner = coarse[MODES : MODES + COARSE, :]
-    mixed[:, 0:128] = near
-    mixed[:, 128:256] = near - exact(inner, exact(square_m, near))
+    mixed[:, 128:256] = (near_rows - exact(exact(near_rows, square_m), inner)).T
     for block in range(SUBS):
         to = ((block % 2) * 8 + block // 2) * 16
         table_even[to : to + 16, :] = mixed[block * MODES : block * MODES + 16, :]
@@ -317,18 +309,24 @@
     project_pair(0, proj, coefficients(all_q), first)
 
     def reduce_all(bufs, value):
-        mates, along_x, along_y, along_z, halves = bufs
+        parts, along_x, along_y, along_z, halves = bufs
         rows = value.shape[0] // 2
-        mates[core, 0] = value[:rows]
-        mates[core, 1] = value[rows:]
-        copy = swap(mates.at[core, 1 - core], mates.at[core, 1 - core], (c, mate))
+        parts[0] = value[:rows]
+        parts[1] = value[rows:]
+        me = 2 * x + core
+        along_x[me] = parts[core]
+        slot = fresh()
+        for peer in x_others[:1] + x_peers[:1] + x_others[1:3] + x_peers[1:] + x_others[3:]:
+            theirs = parts.at[core if peer[1] is s else 1 - core]
+            send(theirs, along_x.at[me], peer, slot)
+        whole = along_x.at[pl.ds(0, 7)]
+        pending.append(lambda: pltpu.make_async_copy(whole, whole, send_sem.at[slot]).wait())
         yield
-        copy.wait_recv()
-        along_x[x] = mates[0, core] + mates[1, core]
-        arrived = share(along_x, x, x_peers)
-        yield
-        arrived.wait()
-        along_y[y] = (along_x[0] + along_x[1]) + (along_x[2] + along_x[3])
+        pltpu.make_async_copy(whole, whole, recv_sem.at[slot]).wait()
+        along_y[y] = (
+            ((along_x[0] + along_x[1]) + (along_x[2] + along_x[3]))
+            + ((along_x[4] + along_x[5]) + (along_x[6] + along_x[7]))
+        )
         arrived = share(along_y, y, y_peers)
         yield
         arrived.wait()
@@ -394,12 +392,6 @@
     def both_parts(value):
         return jnp.concatenate(split(value), axis=0)
 
-    def join_sides(halos, sides_out, copies):
-        for copy in copies:
-            copy.wait_recv()
-        for side in range(4):
-            local[:, part(side)] = sides_out[side] + halos[side]
-
     spread = spread_slots(proj)
     value = product(spread)
     parts = three_parts(value)
@@ -413,8 +405,7 @@
     for copy in near_copies:
         copy.wait_recv()
     arrived = gather_start(all_one, own_part + near_one[0] + near_one[1])
-    next(reduction)
-    join_sides(halo_one, far_one, halo_copies)
+    join_sides(local, halo_one, far_one, halo_copies)
     next(reduction)
     crossed = gather_finish(all_one, arrived)
     next(reduction)
@@ -425,7 +416,6 @@
     next(second)
 
     spread = spread_slots(image_proj)
-    next(second)
     value = product(spread)
     third = reduce_all(sum_c, fold(energy(spread, value)))
     next(third)
@@ -433,34 +423,33 @@
     next(reduction)
     parts = three_parts(value)
     own_part, near_copies = send_moments(parts, out_two, near_two)
-    next(third)
     halo_copies = send_sides(parts, halo_two, far_two)
     both_grams = next(reduction)
     curvature, descent = both_grams[:, :COLS], both_grams[:, COLS:]
+    next(third)
     next(second)
+    for copy in near_copies:
+        copy.wait_recv()
+    arrived = gather_start(all_two, own_part + near_two[0] + near_two[1])
     row = lax.broadcasted_iota(jnp.int32, (COLS, COLS), 0)
     lane = lax.broadcasted_iota(jnp.int32, (COLS, COLS), 1)
     inverse = eliminate(curvature, jnp.where(row == lane, 1.0, 0.0))
+    alpha, alpha_t = exact(inverse, descent), exact(descent, inverse)
     next(third)
-    for copy in near_copies:
-        copy.wait_recv()
-    arrived = gather_start(all_two, own_part + near_two[0] + near_two[1])
-    alpha, alpha_t = exact(inverse, descent), exact(descent, inverse)
     next(second)
-    next(third)
+    join_sides(local, halo_two, far_two, halo_copies)
     norm = unfold(next(second))
     moved = exact(norm, alpha)
     blend = exact(inverse, moved)
     known = exact(alpha_t, exact(norm, blend))
     descent_two = exact(alpha_t, moved) - descent
     crossed = gather_finish(all_two, arrived)
-    join_sides(halo_two, far_two, halo_copies)
+    next(third)
     crossed.wait_recv()
     factors = coefficients(all_two)
     lift = exact(factors[:, :128], moments_map[...])
     basis[place(2), :PAIR] = local[:, :PAIR] - lift
     basis[place(2), PAIR:] = local[:, PAIR:]
-    next(third)
     cubic = unfold(next(third))
 
     curvature_two = exact(alpha_t, exact(cubic, alpha)) - known
@@ -498,7 +487,7 @@
 
     def sums(rows):
         return (
-            vmem(2, 2, rows, 128), vmem(4, rows, 128), vmem(4, rows, 128),
+            vmem(2, rows, 128), vmem(8, rows, 128), vmem(4, rows, 128),
             vmem(8, rows, 128), vmem(2, rows, 128),
         )
 
@@ -519,8 +508,8 @@
             vmem(ROWS, ROWS), vmem(ROWS, ROWS, dtype=BF16), vmem(ROWS, ROWS, dtype=BF16),
             vmem(WIDE, ROWS, dtype=BF16), vmem(ROWS, WIDE, dtype=BF16),
             vmem(8 * MODES, ROWS, dtype=BF16),
-            vmem(COLS, ROWS), vmem(4, COLS, 512), vmem(MODES, 2 * FACE),
-            vmem(2, MODES, 2 * FACE), vmem(COARSE + 3 * MODES, COARSE),
+            vmem(COLS, ROWS), sides, sides, vmem(MODES, 2 * FACE), vmem(2, MODES, SIDE),
+            vmem(2, MODES, SIDE), vmem(COARSE + 3 * MODES, COARSE),
             vmem(4 * MODES, PAIR),
             vmem(8, WIDE), vector, vmem(3 * COLS, WIDE), vector, vector, vector,
             sides, sides, pair, pair, pair, pair, sides, sides,

time: 75.5 us -> 68 us (0.901)
  Pallas kernels: 71.2 us -> 63.7 us
    pallas_call x1, Pallas kernels: 71.2 us -> 63.7 us  [shards(): pl.pallas_call(kernel, out_shape=(out, out), in_specs=[anywhere, anywhere...]
where the time goes in v3:
time: 68 us; the launch traced here: 67.8 us
  Pallas kernels  63.7 us (94%)
  local copies, waits for them, and re-layouts  3.48 us (5%)
    pallas_call x1, Pallas kernels, shards(): pl.pallas_call(kernel, out_shape=(out, out), in_specs=[anywhere, anywhere...  63.7 us
    unnamed x2, local copies, waits for them, and re-layouts  3.48 us

profile of v3, /device:TPU:1, one launch (start us, length us, event | category | flops | bytes accessed | tf_op | source)
XLA Modules:
  0.0 67.8 jit_solution(12002417595462324205)
XLA Ops:
  0.6 63.7 %shard_map.77 = (f32[1,1,64,1408]{3,2,1,0:T(8,128)}, f32[1,1,64,1408]{3,2,1,0:T(8,128)}) custom-call(f32[1,1,1408,1408]{3,2,1,0:T(8,128)} %ops_hbm.1, f32[1,1,64,1408]{3,2,1,0:T(8,128)} %bitcast.3, s32[1,1,4]{2,1,0:T(1,128)} %sizes.1, s32[1,1,1408]{2,1,0:T(1,128)} %map_ref.1, f32[1,1,32,704]{3,2,1,0:T(8,128)} %basis_hbm.1, f32[1,512,512]{2,1,0:T(8,128)} %coarse_hbm.1), custom_call_target="tpu_custom_call" | custom-call | tf_op jit(solution)/shard_map/pallas_call | solution.py:499
  64.3 1.7 %copy.10 = f32[1,1,1408,64]{2,3,1,0:T(8,128)} copy(f32[1,1,1408,64]{2,3,1,0:T(8,128)} %bitcast.5) | data formatting | bytes 720896
  66.0 1.7 %copy.11 = f32[1,1,1408,64]{2,3,1,0:T(8,128)} copy(f32[1,1,1408,64]{2,3,1,0:T(8,128)} %bitcast.4) | data formatting | bytes 720896

commit v4 on v3

--- a/solution.py
+++ b/solution.py
@@ -83,14 +83,14 @@
 
 
 def kernel(
-    ops_hbm, contrib_hbm, sizes, map_ref, basis_hbm, coarse_hbm,
-    sol_hbm, res_hbm,
-    full, high, low, scatter, gather, moments_slots,
+    ops_hbm, contrib_hbm, sizes_hbm, map_hbm, basis_hbm, coarse_hbm,
+    sol_ref, res_ref,
+    sizes, slot_map, full, high, low, scatter, gather, moments_slots,
     own_rhs, halo_q, far_q, own_basis, half_basis, near_basis, coarse, moments_map,
     weights, first, basis, proj, image_proj, local,
     halo_one, halo_two, near_one, near_two, out_one, out_two, far_one, far_two,
     all_q, all_m, all_one, all_two, mixed, table_even, table_odd, dense_m,
-    sum_a, sum_b, sum_c, out_sol, out_res,
+    sum_a, sum_b, sum_c,
     local_sem, send_sem, recv_sem,
 ):
     c, s = lax.axis_index("cluster"), lax.axis_index("sub")
@@ -117,8 +117,10 @@
             coarse_hbm.at[0], coarse.at[pl.ds(MODES, COARSE)], local_sem.at[2]
         ),
         pltpu.make_async_copy(ops_hbm.at[0, 0], full, local_sem.at[3]),
+        pltpu.make_async_copy(map_hbm, slot_map, local_sem.at[6]),
+        pltpu.make_async_copy(sizes_hbm, sizes, local_sem.at[7]),
     ]
-    for load in loads:
+    for load in loads[4:] + loads[:4]:
         load.start()
 
     barrier = pltpu.get_barrier_semaphore()
@@ -129,6 +131,7 @@
             barrier, inc=1, device_id=peer, device_id_type=pl.DeviceIdType.MESH
         )
 
+    loads[5].wait()
     lanes = lax.broadcasted_iota(jnp.int32, (8, SIDE), 1)
     for side in range(4):
         weights[:, part(side)] = jnp.where(lanes < sizes[0, 0, side], SIGNS[side], 0.0)
@@ -179,7 +182,8 @@
         for side in (2, 3, 0, 1)
     ]
 
-    slots = map_ref[0]
+    loads[4].wait()
+    slots = slot_map[0]
     slots = slots + (SIDE - FACE) * (
         (slots >= FACE).astype(jnp.int32)
         + (slots >= 2 * FACE).astype(jnp.int32)
@@ -193,24 +197,6 @@
         return carry
 
     lax.fori_loop(0, WIDE // 128, fill_scatter, 0)
-    columns = lax.broadcasted_iota(jnp.int32, (128, 128), 1).astype(F32)
-    for step in range(ROWS // 128):
-        piece = slots[:, step * 128 : (step + 1) * 128].astype(F32)
-        tall = jnp.broadcast_to(piece, (128, 128)).T
-        for tile in range(WIDE // 128):
-            gather[step * 128 : (step + 1) * 128, tile * 128 : (tile + 1) * 128] = (
-                jnp.where(tall == columns + float(tile * 128), 1.0, 0.0).astype(BF16)
-            )
-
-    loads[3].wait()
-
-    def split_rows(step, carry):
-        rows = pl.ds(pl.multiple_of(step * 64, 64), 64)
-        high[rows, :], low[rows, :] = split(full[rows, :])
-        return carry
-
-    lax.fori_loop(0, ROWS // 64, split_rows, 0)
-
     weight_low, weight_high = weights[0:1, part(0)], weights[0:1, part(1)]
     empty = jnp.zeros((MODES, SIDE), F32)
     moments_map[MODES : 2 * MODES, part(0)] = half_basis[0] * weight_low
@@ -231,6 +217,27 @@
         arrived.wait()
         return swap(buffer.at[core], buffer.at[core], (c, mate))
 
+    m_own = exact(moments_map[MODES : 2 * MODES, :], moments_map[...], NT)
+    m_own = jnp.concatenate(
+        [0.5 * m_own[:, MODES : 2 * MODES], m_own[:, 2 * MODES : 3 * MODES]], axis=1
+    )
+    m_arrived = gather_start(all_m, fold(m_own))
+
+    columns = lax.broadcasted_iota(jnp.int32, (128, 128), 1).astype(F32)
+    for step in range(ROWS // 128):
+        piece = slots[:, step * 128 : (step + 1) * 128].astype(F32)
+        tall = jnp.broadcast_to(piece, (128, 128)).T
+        for tile in range(WIDE // 128):
+            gather[step * 128 : (step + 1) * 128, tile * 128 : (tile + 1) * 128] = (
+                jnp.where(tall == columns + float(tile * 128), 1.0, 0.0).astype(BF16)
+            )
+
+    map_high, map_low = split(moments_map[...] * weights[0:1, :PAIR])
+    spread = single(jnp.concatenate([map_high, map_low], axis=0), scatter[:PAIR, :])
+    map_high, map_low = split(spread[: 4 * MODES] + spread[4 * MODES :])
+    moments_slots[: 4 * MODES] = map_high
+    moments_slots[4 * MODES :] = map_low
+
     def join_sides(target, halos, sides_out, copies):
         for copy in copies:
             copy.wait_recv()
@@ -240,18 +247,12 @@
     join_sides(first, halo_q, far_q, rhs_copies)
     q_moments = exact(moments_map[MODES : 2 * MODES, :], first[:, :PAIR], NT)
     q_arrived = gather_start(all_q, fold(q_moments))
-    m_own = exact(moments_map[MODES : 2 * MODES, :], moments_map[...], NT)
-    m_own = jnp.concatenate(
-        [0.5 * m_own[:, MODES : 2 * MODES], m_own[:, 2 * MODES : 3 * MODES]], axis=1
-    )
-    m_arrived = gather_start(all_m, fold(m_own))
-
-    map_high, map_low = split(moments_map[...] * weights[0:1, :PAIR])
-    spread = single(jnp.concatenate([map_high, map_low], axis=0), scatter[:PAIR, :])
-    map_high, map_low = split(spread[: 4 * MODES] + spread[4 * MODES :])
-    moments_slots[: 4 * MODES] = map_high
-    moments_slots[4 * MODES :] = map_low
-
+    def split_rows(step, carry):
+        rows = pl.ds(pl.multiple_of(step * 64, 64), 64)
+        high[rows, :], low[rows, :] = split(full[rows, :])
+        return carry
+
+    m_crossed = gather_finish(all_m, m_arrived)
     loads[2].wait()
     coarse[0:MODES, :] = jnp.zeros((MODES, COARSE), F32)
     coarse[MODES + COARSE :, :] = jnp.zeros((2 * MODES, COARSE), F32)
@@ -259,8 +260,8 @@
     mixed[:, 0:128] = near_rows.T
     dense_m[...] = jnp.zeros((COARSE, COARSE + 128), F32)
 
-    q_crossed = gather_finish(all_q, q_arrived)
-    m_crossed = gather_finish(all_m, m_arrived)
+    loads[3].wait()
+    lax.fori_loop(0, ROWS // 128, split_rows, 0)
     m_crossed.wait_recv()
     lane = lax.broadcasted_iota(jnp.int32, (MODES, 128), 1)
     blank = jnp.zeros((MODES, 64), F32)
@@ -305,6 +306,8 @@
         basis[place(which), PAIR:] = source[:, PAIR:]
         value_proj[:, PAIR:] = source[:, PAIR:]
 
+    q_crossed = gather_finish(all_q, q_arrived)
+    lax.fori_loop(ROWS // 128, ROWS // 64, split_rows, 0)
     q_crossed.wait_recv()
     project_pair(0, proj, coefficients(all_q), first)
 
@@ -454,8 +457,8 @@
 
     curvature_two = exact(alpha_t, exact(cubic, alpha)) - known
     alpha_two = eliminate(curvature_two, descent_two)
-    outer = (alpha + exact(blend, alpha_two)).T
-    cross = exact(alpha, alpha_two).T
+    both = exact(jnp.concatenate([blend, alpha], axis=0), alpha_two)
+    outer, cross = (alpha + both[:COLS]).T, both[COLS:].T
     none = jnp.zeros((COLS, COLS), F32)
     mix = jnp.concatenate(
         [
@@ -467,18 +470,21 @@
     for side in range(4):
         result = exact(mix, basis[:, part(side)])
         at = slice(side * FACE, (side + 1) * FACE)
-        out_sol[:, at] = result[:COLS, :FACE]
-        out_res[:, at] = (basis[place(0), part(side)] + result[COLS:])[:, :FACE]
-    stores = [
-        pltpu.make_async_copy(out_sol, sol_hbm.at[0, 0], local_sem.at[4]),
-        pltpu.make_async_copy(out_res, res_hbm.at[0, 0], local_sem.at[5]),
-    ]
-    for store in stores:
-        store.start()
+        sol_ref[0, 0, :, at] = result[:COLS, :FACE]
+        res_ref[0, 0, :, at] = (basis[place(0), part(side)] + result[COLS:])[:, :FACE]
     for wait in pending:
         wait()
-    for store in stores:
-        store.wait()
+
+
+def store(sol_in, res_in, sol_out, res_out, sem):
+    copies = [
+        pltpu.make_async_copy(sol_in, sol_out, sem.at[0]),
+        pltpu.make_async_copy(res_in, res_out, sem.at[1]),
+    ]
+    for copy in copies:
+        copy.start()
+    for copy in copies:
+        copy.wait()
 
 
 def shards(dual_ops, contributions, block_sizes, mult_map, coarse_basis, coarse_inverse):
@@ -495,16 +501,17 @@
     moments = vmem(2, 8, 16, 128)
     sides, pair = vmem(4, COLS, SIDE), vmem(2, 16, 128)
     anywhere = pl.BlockSpec(memory_space=pl.ANY)
+    near_spec = pl.BlockSpec(memory_space=pltpu.VMEM)
     out = jax.ShapeDtypeStruct((1, 1, COLS, ROWS), F32)
     results = pl.pallas_call(
         kernel,
         out_shape=(out, out),
         in_specs=[
-            anywhere, anywhere, pl.BlockSpec(memory_space=pltpu.SMEM),
-            pl.BlockSpec(memory_space=pltpu.VMEM), anywhere, anywhere,
+            anywhere, anywhere, anywhere, anywhere, anywhere, anywhere,
         ],
-        out_specs=(anywhere, anywhere),
+        out_specs=(near_spec, near_spec),
         scratch_shapes=[
+            pltpu.SMEM((1, 1, 4), jnp.int32), vmem(1, 1, ROWS, dtype=jnp.int32),
             vmem(ROWS, ROWS), vmem(ROWS, ROWS, dtype=BF16), vmem(ROWS, ROWS, dtype=BF16),
             vmem(WIDE, ROWS, dtype=BF16), vmem(ROWS, WIDE, dtype=BF16),
             vmem(8 * MODES, ROWS, dtype=BF16),
@@ -515,17 +522,22 @@
             sides, sides, pair, pair, pair, pair, sides, sides,
             moments, moments, moments, moments,
             vmem(COARSE, 256), vmem(256, 256), vmem(256, 256), vmem(COARSE, COARSE + 128),
-            sums(32), sums(16), sums(16), vmem(COLS, ROWS), vmem(COLS, ROWS),
-            pltpu.SemaphoreType.DMA((6,)), pltpu.SemaphoreType.DMA((64,)),
+            sums(32), sums(16), sums(16),
+            pltpu.SemaphoreType.DMA((8,)), pltpu.SemaphoreType.DMA((64,)),
             pltpu.SemaphoreType.DMA((64,)),
         ],
         compiler_params=pltpu.CompilerParams(
-            collective_id=0, has_side_effects=True, vmem_limit_bytes=60 * 1024 * 1024
+            collective_id=0, has_side_effects=True, vmem_limit_bytes=55_500_000
         ),
     )(
         dual_ops, jnp.swapaxes(contributions, 2, 3), block_sizes, mult_map,
         coarse_basis, coarse_inverse,
     )
+    results = pl.pallas_call(
+        store, out_shape=(out, out), in_specs=[near_spec, near_spec],
+        out_specs=(anywhere, anywhere), scratch_shapes=[pltpu.SemaphoreType.DMA((2,))],
+        compiler_params=pltpu.CompilerParams(vmem_limit_bytes=4 * 1024 * 1024),
+    )(*results)
     return tuple(jnp.swapaxes(result, 2, 3) for result in results)
 
 

time: 68 us -> 64.8 us (0.953)
  Pallas kernels: 63.7 us -> 61.6 us
  local copies, waits for them, and re-layouts: 3.48 us -> 2.23 us
    pallas_call x1, Pallas kernels: 63.7 us -> 60.7 us  [shards(): pl.pallas_call(kernel, out_shape=(out, out), in_specs=[anywhere, anywhere...]
    unnamed x2 -> x6, local copies, waits for them, and re-layouts: 3.48 us -> 2.23 us
    pallas_call x0 -> x1, Pallas kernels: none -> 0.87 us  [shards(): pl.pallas_call(store, out_shape=(out, out), in_specs=[near_spec, near_spe...]
where the time goes in v4:
time: 64.8 us; the launch traced here: 64.7 us
  Pallas kernels  61.6 us (95%)
  local copies, waits for them, and re-layouts  2.23 us (3%)
  between operations  0.83 us (1%)
    pallas_call x1, Pallas kernels, shards(): pl.pallas_call(kernel, out_shape=(out, out), in_specs=[anywhere, anywhere...  60.7 us
    unnamed x6, local copies, waits for them, and re-layouts  2.23 us

profile of v4, /device:TPU:1, one launch (start us, length us, event | category | flops | bytes accessed | tf_op | source)
XLA Modules:
  0.0 64.7 jit_solution(2695471424856064646)
XLA Ops:
  0.6 0.0 copy-start
  0.6 0.9 %copy-done = f32[1,1,32,704]{3,2,1,0:T(8,128)S(1)} copy-done((f32[1,1,32,704]{3,2,1,0:T(8,128)S(1)}, f32[1,1,32,704]{3,2,1,0:T(8,128)}, u32[]{:S(2)}) %copy-start) | copy-done | bytes 90136
  1.5 0.0 copy-start.1
  1.5 0.7 %copy-done.1 = s32[1,1,1408]{2,1,0:T(1,128)S(1)} copy-done((s32[1,1,1408]{2,1,0:T(1,128)S(1)}, s32[1,1,1408]{2,1,0:T(1,128)}, u32[]{:S(2)}) %copy-start.1) | copy-done | bytes 5656
  2.2 0.0 copy-start.2
  2.2 0.7 %copy-done.2 = s32[1,1,4]{2,1,0:T(1,128)S(1)} copy-done((s32[1,1,4]{2,1,0:T(1,128)S(1)}, s32[1,1,4]{2,1,0:T(1,128)}, u32[]{:S(2)}) %copy-start.2) | copy-done | bytes 40
  2.9 60.7 %shard_map.77 = (f32[1,1,64,1408]{3,2,1,0:T(8,128)S(1)}, f32[1,1,64,1408]{3,2,1,0:T(8,128)S(1)}) custom-call(f32[1,1,1408,1408]{3,2,1,0:T(8,128)} %ops_hbm.1, f32[1,1,64,1408]{3,2,1,0:T(8,128)} %bitcast.3, s32[1,1,4]{2,1,0:T(1,128)S(1)} %copy-done.2, s32[1,1,1408]{2,1,0:T(1,128)S(1)} %copy-done.1, f32[1,1,32,704]{3,2,1,0:T(8,128)S(1)} %copy-done, ...), custom_call_target="tpu_custom_call" | custom-call | tf_op jit(solution)/shard_map/pallas_call | solution.py:506
  63.6 0.9 %shard_map.78 = (f32[1,1,64,1408]{3,2,1,0:T(8,128)}, f32[1,1,64,1408]{3,2,1,0:T(8,128)}) custom-call(f32[1,1,64,1408]{3,2,1,0:T(8,128)S(1)} %get-tuple-element.6.sol_in, f32[1,1,64,1408]{3,2,1,0:T(8,128)S(1)} %get-tuple-element.7.res_in), custom_call_target="tpu_custom_call" | custom-call | tf_op jit(solution)/shard_map/pallas_call | solution.py:536
Async XLA Ops:
  0.6 0.9 %copy-start = (f32[1,1,32,704]{3,2,1,0:T(8,128)S(1)}, f32[1,1,32,704]{3,2,1,0:T(8,128)}, u32[]{:S(2)}) copy-start(f32[1,1,32,704]{3,2,1,0:T(8,128)} %basis_hbm.1) | copy-start | bytes 270340
  1.5 0.7 %copy-start.1 = (s32[1,1,1408]{2,1,0:T(1,128)S(1)}, s32[1,1,1408]{2,1,0:T(1,128)}, u32[]{:S(2)}) copy-start(s32[1,1,1408]{2,1,0:T(1,128)} %map_hbm.1) | copy-start | bytes 16900
  2.2 0.7 %copy-start.2 = (s32[1,1,4]{2,1,0:T(1,128)S(1)}, s32[1,1,4]{2,1,0:T(1,128)}, u32[]{:S(2)}) copy-start(s32[1,1,4]{2,1,0:T(1,128)} %sizes_hbm.1) | copy-start | bytes 52

commit v5 on v4

--- a/solution.py
+++ b/solution.py
@@ -84,13 +84,13 @@
 
 def kernel(
     ops_hbm, contrib_hbm, sizes_hbm, map_hbm, basis_hbm, coarse_hbm,
-    sol_ref, res_ref,
+    sol_hbm, res_hbm,
     sizes, slot_map, full, high, low, scatter, gather, moments_slots,
     own_rhs, halo_q, far_q, own_basis, half_basis, near_basis, coarse, moments_map,
     weights, first, basis, proj, image_proj, local,
     halo_one, halo_two, near_one, near_two, out_one, out_two, far_one, far_two,
     all_q, all_m, all_one, all_two, mixed, table_even, table_odd, dense_m,
-    sum_a, sum_b, sum_c,
+    sum_a, sum_b, sum_c, out_sol, out_res,
     local_sem, send_sem, recv_sem,
 ):
     c, s = lax.axis_index("cluster"), lax.axis_index("sub")
@@ -470,20 +470,41 @@
     for side in range(4):
         result = exact(mix, basis[:, part(side)])
         at = slice(side * FACE, (side + 1) * FACE)
-        sol_ref[0, 0, :, at] = result[:COLS, :FACE]
-        res_ref[0, 0, :, at] = (basis[place(0), part(side)] + result[COLS:])[:, :FACE]
+        out_sol[:, at] = result[:COLS, :FACE]
+        out_res[:, at] = (basis[place(0), part(side)] + result[COLS:])[:, :FACE]
+    stores = [
+        pltpu.make_async_copy(out_sol, sol_hbm.at[0, 0], local_sem.at[4]),
+        pltpu.make_async_copy(out_res, res_hbm.at[0, 0], local_sem.at[5]),
+    ]
+    for store in stores:
+        store.start()
     for wait in pending:
         wait()
-
-
-def store(sol_in, res_in, sol_out, res_out, sem):
-    copies = [
-        pltpu.make_async_copy(sol_in, sol_out, sem.at[0]),
-        pltpu.make_async_copy(res_in, res_out, sem.at[1]),
-    ]
-    for copy in copies:
+    for store in stores:
+        store.wait()
+
+
+def store(sol_in, res_in, sol_out, res_out, held, in_sem, out_sem):
+    loads, stores = [], []
+    for which, (source, target) in enumerate(((sol_in, sol_out), (res_in, res_out))):
+        for quarter in range(4):
+            at, slot = pl.ds(16 * quarter, 16), 4 * which + quarter
+            loads.append(
+                pltpu.make_async_copy(
+                    source.at[0, 0, at], held.at[which, at], in_sem.at[slot]
+                )
+            )
+            stores.append(
+                pltpu.make_async_copy(
+                    held.at[which, at], target.at[0, 0, at], out_sem.at[slot]
+                )
+            )
+    for load in loads:
+        load.start()
+    for load, copy in zip(loads, stores):
+        load.wait()
         copy.start()
-    for copy in copies:
+    for copy in stores:
         copy.wait()
 
 
@@ -501,7 +522,6 @@
     moments = vmem(2, 8, 16, 128)
     sides, pair = vmem(4, COLS, SIDE), vmem(2, 16, 128)
     anywhere = pl.BlockSpec(memory_space=pl.ANY)
-    near_spec = pl.BlockSpec(memory_space=pltpu.VMEM)
     out = jax.ShapeDtypeStruct((1, 1, COLS, ROWS), F32)
     results = pl.pallas_call(
         kernel,
@@ -509,7 +529,7 @@
         in_specs=[
             anywhere, anywhere, anywhere, anywhere, anywhere, anywhere,
         ],
-        out_specs=(near_spec, near_spec),
+        out_specs=(anywhere, anywhere),
         scratch_shapes=[
             pltpu.SMEM((1, 1, 4), jnp.int32), vmem(1, 1, ROWS, dtype=jnp.int32),
             vmem(ROWS, ROWS), vmem(ROWS, ROWS, dtype=BF16), vmem(ROWS, ROWS, dtype=BF16),
@@ -522,21 +542,24 @@
             sides, sides, pair, pair, pair, pair, sides, sides,
             moments, moments, moments, moments,
             vmem(COARSE, 256), vmem(256, 256), vmem(256, 256), vmem(COARSE, COARSE + 128),
-            sums(32), sums(16), sums(16),
+            sums(32), sums(16), sums(16), vmem(COLS, ROWS), vmem(COLS, ROWS),
             pltpu.SemaphoreType.DMA((8,)), pltpu.SemaphoreType.DMA((64,)),
             pltpu.SemaphoreType.DMA((64,)),
         ],
         compiler_params=pltpu.CompilerParams(
-            collective_id=0, has_side_effects=True, vmem_limit_bytes=55_500_000
+            collective_id=0, has_side_effects=True, vmem_limit_bytes=60 * 1024 * 1024
         ),
     )(
         dual_ops, jnp.swapaxes(contributions, 2, 3), block_sizes, mult_map,
         coarse_basis, coarse_inverse,
     )
     results = pl.pallas_call(
-        store, out_shape=(out, out), in_specs=[near_spec, near_spec],
-        out_specs=(anywhere, anywhere), scratch_shapes=[pltpu.SemaphoreType.DMA((2,))],
-        compiler_params=pltpu.CompilerParams(vmem_limit_bytes=4 * 1024 * 1024),
+        store, out_shape=(out, out), in_specs=[anywhere, anywhere],
+        out_specs=(anywhere, anywhere),
+        scratch_shapes=[
+            vmem(2, COLS, ROWS), pltpu.SemaphoreType.DMA((8,)), pltpu.SemaphoreType.DMA((8,)),
+        ],
+        compiler_params=pltpu.CompilerParams(vmem_limit_bytes=60 * 1024 * 1024),
     )(*results)
     return tuple(jnp.swapaxes(result, 2, 3) for result in results)
 

time: 64.8 us -> 64.6 us (level)
  local copies, waits for them, and re-layouts: 2.23 us -> 0 us
  Pallas kernels: 61.6 us -> 63.6 us
    unnamed x6 -> x0, local copies, waits for them, and re-layouts: 2.23 us -> none
    pallas_call x1, Pallas kernels: 0.87 us -> 1.96 us  [shards(): pl.pallas_call(store, out_shape=(out, out), in_specs=[anywhere, anywhere]...]
    pallas_call x1, Pallas kernels: 60.7 us -> 61.7 us  [shards(): pl.pallas_call(kernel, out_shape=(out, out), in_specs=[anywhere, anywhere...]
where the time goes in v5:
time: 64.6 us; the launch traced here: 64.5 us
  Pallas kernels  63.6 us (98%)
  between operations  0.82 us (1%)
    pallas_call x1, Pallas kernels, shards(): pl.pallas_call(kernel, out_shape=(out, out), in_specs=[anywhere, anywhere...  61.7 us
    pallas_call x1, Pallas kernels, shards(): pl.pallas_call(store, out_shape=(out, out), in_specs=[anywhere, anywhere]...  1.96 us

profile of v5, /device:TPU:1, one launch (start us, length us, event | category | flops | bytes accessed | tf_op | source)
XLA Modules:
  0.0 64.5 jit_solution(16227169107578084450)
XLA Ops:
  0.6 61.7 %shard_map.77 = (f32[1,1,64,1408]{3,2,1,0:T(8,128)}, f32[1,1,64,1408]{3,2,1,0:T(8,128)}) custom-call(f32[1,1,1408,1408]{3,2,1,0:T(8,128)} %ops_hbm.1, f32[1,1,64,1408]{3,2,1,0:T(8,128)} %bitcast.3, s32[1,1,4]{2,1,0:T(1,128)} %sizes_hbm.1, s32[1,1,1408]{2,1,0:T(1,128)} %map_hbm.1, f32[1,1,32,704]{3,2,1,0:T(8,128)} %basis_hbm.1, f32[1,512,512]{2,1,0:T(8,128)} %coarse_hbm.1), custom_call_target="tpu_custom_call" | custom-call | tf_op jit(solution)/shard_map/pallas_call | solution.py:526
  62.3 2.0 %shard_map.78 = (f32[1,1,64,1408]{3,2,1,0:T(8,128)}, f32[1,1,64,1408]{3,2,1,0:T(8,128)}) custom-call(f32[1,1,64,1408]{3,2,1,0:T(8,128)} %get-tuple-element.6.sol_in, f32[1,1,64,1408]{3,2,1,0:T(8,128)} %get-tuple-element.7.res_in), custom_call_target="tpu_custom_call" | custom-call | tf_op jit(solution)/shard_map/pallas_call | solution.py:556
